TPU v7x, 128 devices: a whole 4x4x4 slice. The times are simulated.
128 devices in a mesh: section: 2 (over z_lo), patch: 4 (over y), shard: 16 (over z_hi, x, core).
Axes of the slice: x: 4, y: 4, z: 4 (z_hi: 2, z_lo: 2; z = z_hi * 2 + z_lo), core: 2. Of those that a mesh axis runs over, the one named last changes fastest.
Arguments:
- hidden: bfloat16 [32, 1024, 2432], P('shard', 'patch'), may hold values from -6 to 6
- text_kv: bfloat16 [2, 32, 154, 2432], P('section', 'shard'), may hold values from -6 to 6, as said below
- stale_kv: bfloat16 [2, 32, 1024, 2432], P('section', 'shard', 'patch'), may hold values from -6 to 6, as said below
- modulation: float32 [2, 32, 3, 2432], P('section', 'shard'), may hold values from -3 to 3
- score_gain: float32 [2, 64], P('section'), may hold values from 1.5 to 4
- qkv_weight: bfloat16 [2, 2432, 3648], P('section', 'shard'), may hold values from -0.125 to 0.125
- out_weight: bfloat16 [2, 1216, 2432], P('section', None, 'shard'), may hold values from -0.15625 to 0.15625
- final_mod: float32 [32, 2, 2432], P('shard'), may hold values from -3 to 3
- final_weight: bfloat16 [2432, 64], replicated, may hold values from -0.125 to 0.125
- latent: float32 [32, 1024, 64], P('shard', ('patch', 'section')), may hold values from -6 to 6
- step_index: int32 [32], P('shard'), may hold values from 0 to 27
Outputs:
- new_kv: bfloat16 [2, 32, 1024, 2432], P('section', 'shard', 'patch')
- latent_next: float32 [32, 1024, 64], P('shard', ('patch', 'section'))
- denoised: float32 [32, 1024, 64], P('shard', ('patch', 'section'))
Inputs may be any that keep to these rules, and one draw needn't show every extreme that they name: `text_kv`: in every row the first 1216 columns are 19 heads of 64 key features, each head with mean square one up to bfloat16 rounding. `stale_kv`: in every row the first 1216 columns are 19 heads of 64 key features, each head with mean square one up to bfloat16 rounding.
All inputs are finite; a program needn't handle non-finite values.
Results may differ from a plain program's by a relative error of at most 0.008.
Values may be sent and summed in bfloat16 or wider, within the bound.
No kernel may reach another device: no remote copies, remote signals or barrier semaphores. Data moves between devices by JAX's collectives and lax.ppermute only.
A program may use at most 192 MiB of HBM per device.

v0:
```python
import math

import jax
import jax.numpy as jnp
from jax import lax
from jax.experimental import pallas as pl
from jax.experimental.pallas import tpu as pltpu
from jax.sharding import PartitionSpec as P

HEAD = 64
NSTEPS = 28
D = 2432
HW = 1216
ROWS = 256
TXT = 154
TXT_PAD = 160
KEYS = 4 * ROWS + TXT_PAD
BLK = 304
ZC = 1152
XC = D - ZC
WIDE = 1280
LANE = 128
NT = 256

eps_norm = 1e-06
flow_shift = 3.0


def sigma_of(step):
    s = 1.0 - step.astype(jnp.float32) / NSTEPS
    return flow_shift * s / (1.0 + (flow_shift - 1.0) * s)


def shard_pairs(flip_z=0, dx=0, flip_core=0):
    pairs = []
    for z in range(2):
        for x in range(4):
            for c in range(2):
                src = z * 8 + x * 2 + c
                dst = (z ^ flip_z) * 8 + ((x + dx) % 4) * 2 + (c ^ flip_core)
                pairs.append((src, dst))
    return pairs


def ring_pairs(step):
    return [(i, (i + step) % 4) for i in range(4)]


def x_shift(value, dx):
    return lax.ppermute(value, "shard", shard_pairs(dx=dx))


def z_flip(value):
    return lax.ppermute(value, "shard", shard_pairs(flip_z=1))


def core_flip(value):
    return lax.ppermute(value, "shard", shard_pairs(flip_core=1))


def y_shift(value, dy):
    return lax.ppermute(value, "patch", ring_pairs(dy))


def x_relay(value):
    pairs = []
    for z in range(2):
        for x in range(4):
            for c in range(2):
                dx = 1 if c == 0 else -1
                pairs.append((z * 8 + x * 2 + c, z * 8 + ((x + dx) % 4) * 2 + c))
    return lax.ppermute(value, "shard", pairs)


def y_relay(value):
    pairs = []
    for y in range(4):
        for k in range(16):
            dy = 1 if k % 2 == 0 else -1
            pairs.append((y * 16 + k, ((y + dy) % 4) * 16 + k))
    return lax.ppermute(value, ("patch", "shard"), pairs)


def after(value, *earlier):
    return lax.optimization_barrier((value, *earlier))[0]


def group_scale(p, ones_ref):
    total = jnp.dot(
        (p * p).astype(jnp.bfloat16), ones_ref[...], preferred_element_type=jnp.float32
    )
    return lax.rsqrt(total * (1.0 / HEAD) + eps_norm)


def norm_rows(src_ref, shift_ref, scale_ref, dst_ref):
    step = 32

    def body(i, _):
        r = pl.multiple_of(i * step, step)
        xf = src_ref[pl.ds(r, step), :].astype(jnp.float32)
        mean = jnp.mean(xf, -1, keepdims=True)
        cent = xf - mean
        var = jnp.mean(cent * cent, -1, keepdims=True)
        out = cent * lax.rsqrt(var + eps_norm) * (1.0 + scale_ref[...]) + shift_ref[...]
        dst_ref[pl.ds(r, step), :] = out.astype(jnp.bfloat16)
        return 0

    lax.fori_loop(0, ROWS // step, body, 0)


def layer_kernel(final, req, *refs):
    sc, x_hbm, mod_ref, gain_ref = refs[:4]
    mine = refs[4:13]
    theirs = refs[13:22]
    stale = refs[22:25]
    text_ref = refs[25]
    refs = refs[26:]
    mod_ref = mod_ref.at[req]
    if final:
        fmod_ref, fw_ref, early_ref = refs[0].at[req], refs[1], refs[2]
        refs = refs[4:] if req else refs[3:]
        vel_ref, fresh_ref = refs[:2]
        fresh_ref = fresh_ref.at[req]
        w_kv, w_q, w_o, kv, normed, qbuf, attn, ones, x_ref, sems, x_out = refs[2:]
    else:
        x_hbm = x_hbm.at[req]
        x_out, fresh_ref = refs[:2]
        w_kv, w_q, w_o, kv, normed, qbuf, attn, ones, x_ref, sems = refs[2:]
    row_of = lambda slot, j: pl.multiple_of(sc[1 + slot * 4 + j], 16)

    def put(ref, at, col, count, dst, slot, j, dst_col, sem):
        pltpu.make_async_copy(
            ref.at[pl.ds(at, BLK), pl.ds(col, count)],
            dst.at[pl.ds(row_of(slot, j), BLK), pl.ds(dst_col, count)],
            sem,
        ).start()

    def spread_z(pieces, dst, sem):
        put(pieces[0], 0, 0, ZC, dst, 0, 0, 0, sem)
        put(pieces[1], 0, 0, ZC, dst, 1, 0, 0, sem)
        for j, ref in enumerate(pieces[4:7]):
            for slot in range(2):
                put(ref, slot * BLK, 0, ZC, dst, slot, j + 1, 0, sem)

    def spread_x(pieces, count, dst, dst_col, sem):
        for slot in range(2):
            near, two, far = pieces[slot], pieces[(2, 7)[slot]], pieces[(3, 8)[slot]]
            put(near, 0, ZC, count, dst, slot, 0, dst_col, sem)
            for j in range(2):
                put(two, j * BLK, 0, count, dst, slot, j + 1, dst_col, sem)
            put(far, 0, 0, count, dst, slot, 3, dst_col, sem)

    def by_core(step):
        @pl.when(sc[0] == 0)
        def _():
            step(mine, theirs)

        @pl.when(sc[0] != 0)
        def _():
            step(theirs, mine)

    def fetch_kv_z(kv_pieces, oq_pieces):
        spread_z(kv_pieces, w_kv, sems.at[0])

    def fetch_kv_x(kv_pieces, oq_pieces):
        spread_x(kv_pieces, XC, w_kv, ZC, sems.at[1])

    def fetch_q(kv_pieces, oq_pieces):
        spread_z(oq_pieces, w_q, sems.at[2])
        spread_x(oq_pieces, WIDE - ZC, w_q, ZC, sems.at[2])

    def fetch_out(kv_pieces, oq_pieces):
        spread_x(oq_pieces, XC, w_o, 0, sems.at[4])

    def fetch_keys():
        for j, ref in enumerate((*stale, text_ref)):
            count = ROWS if j < 3 else TXT_PAD
            pltpu.make_async_copy(
                ref.at[req], kv.at[pl.ds((j + 1) * ROWS, count), :], sems.at[3]
            ).start()

    def wait(dst, sem):
        pltpu.make_async_copy(dst, dst, sem).wait()

    pltpu.make_async_copy(x_hbm, x_ref, sems.at[5]).start()
    by_core(fetch_kv_z)
    wait(x_ref, sems.at[5])

    norm_rows(x_ref, mod_ref.at[0:1, :], mod_ref.at[1:2, :], normed)
    gi = lax.broadcasted_iota(jnp.int32, (NT, NT), 0) // HEAD
    gj = lax.broadcasted_iota(jnp.int32, (NT, NT), 1) // HEAD
    ones[...] = jnp.where(gi == gj, 1.0, 0.0).astype(jnp.bfloat16)

    by_core(fetch_kv_x)
    wait(w_kv.at[:, pl.ds(0, ZC)], sems.at[0])
    by_core(fetch_q)

    def key_block(j, _):
        c = pl.multiple_of(j * NT, NT)
        p = jnp.dot(normed[...], w_kv[:, pl.ds(c, NT)], preferred_element_type=jnp.float32)
        col = lax.broadcasted_iota(jnp.int32, (ROWS, NT), 1) + c
        out = p * jnp.where(col < HW, group_scale(p, ones), 1.0)
        kv[pl.ds(0, ROWS), pl.ds(c, NT)] = out.astype(jnp.bfloat16)
        return 0

    lax.fori_loop(0, ZC // NT, key_block, 0)
    wait(w_kv.at[:, pl.ds(ZC, XC)], sems.at[1])
    fetch_keys()
    key_block(ZC // NT, 0)
    vw = 384

    def value_block(j, _):
        c = pl.multiple_of(WIDE + j * vw, LANE)
        p = jnp.dot(normed[...], w_kv[:, pl.ds(c, vw)], preferred_element_type=jnp.float32)
        kv[pl.ds(0, ROWS), pl.ds(c, vw)] = p.astype(jnp.bfloat16)
        return 0

    lax.fori_loop(0, (D - WIDE) // vw, value_block, 0)
    new_rows = kv.at[pl.ds(0, ROWS), :]
    spare = w_kv.at[pl.ds(0, ROWS), :]
    if final:

        @pl.when(sc[9] == 0)
        def _():
            pltpu.make_async_copy(early_ref, spare, sems.at[6]).start()

    else:
        pltpu.make_async_copy(new_rows, fresh_ref, sems.at[6]).start()
    wait(w_q, sems.at[2])
    by_core(fetch_out)

    def query_block(j, _):
        c = pl.multiple_of(j * NT, NT)
        p = jnp.dot(normed[...], w_q[:, pl.ds(c, NT)], preferred_element_type=jnp.float32)
        q = p * group_scale(p, ones) * gain_ref[:, pl.ds(c, NT)]
        qbuf[:, pl.ds(c, NT)] = q.astype(jnp.bfloat16)
        return 0

    lax.fori_loop(0, WIDE // NT, query_block, 0)
    wait(kv.at[pl.ds(ROWS, KEYS - ROWS), :], sems.at[3])

    low = lax.broadcasted_iota(jnp.int32, (ROWS, LANE), 1) < HEAD
    zero = jnp.zeros((ROWS, LANE), jnp.bfloat16)
    chunks = [(i * ROWS, ROWS) for i in range(4)] + [(4 * ROWS, TXT_PAD)]
    contract = (((1,), (1,)), ((), ()))
    one_rows = jnp.ones((ROWS, LANE), jnp.bfloat16)
    text_rows = jnp.where(
        lax.broadcasted_iota(jnp.int32, (TXT_PAD, LANE), 0) < TXT, 1.0, 0.0
    ).astype(jnp.bfloat16)

    def attend(q, key_of, vc):
        acc = None
        for start, count in chunks:
            v = kv[pl.ds(start, count), pl.ds(vc, LANE)]
            s = lax.dot_general(
                q, key_of(start, count), contract, preferred_element_type=jnp.float32
            )
            w = jnp.exp(s).astype(jnp.bfloat16)
            v_one = jnp.concatenate([v, one_rows if count == ROWS else text_rows], 1)
            part = jnp.dot(w, v_one, preferred_element_type=jnp.float32)
            acc = part if acc is None else acc + part
        return acc[:, :LANE] / acc[:, LANE:]

    def pair(j, _):
        c = pl.multiple_of(j * LANE, LANE)
        n = pl.multiple_of(c + LANE, LANE)
        q_c, q_n = qbuf[:, pl.ds(c, LANE)], qbuf[:, pl.ds(n, LANE)]
        q = jnp.concatenate([jnp.where(low, zero, q_c), jnp.where(low, q_n, zero)], 0)

        def key_of(start, count):
            return jnp.where(
                low[:count], kv[pl.ds(start, count), pl.ds(n, LANE)],
                kv[pl.ds(start, count), pl.ds(c, LANE)],
            )

        out = attend(q, key_of, pl.multiple_of(c + 10 * LANE, LANE))
        out = jnp.where(low, out[:ROWS], out[ROWS:])
        attn[:, pl.ds(n, LANE)] = out.astype(jnp.bfloat16)
        return 0

    lax.fori_loop(0, 9, pair, 0, unroll=3)
    first = attend(
        jnp.where(low, qbuf[:, pl.ds(0, LANE)], zero),
        lambda start, count: kv[pl.ds(start, count), pl.ds(0, LANE)],
        9 * LANE,
    )
    attn[:, pl.ds(0, LANE)] = jnp.where(low, 0.0, first).astype(jnp.bfloat16)

    if final:

        @pl.when(sc[9] == 0)
        def _():
            wait(spare, sems.at[6])
            pltpu.make_async_copy(spare, fresh_ref, sems.at[6]).start()

        @pl.when(sc[9] != 0)
        def _():
            pltpu.make_async_copy(new_rows, fresh_ref, sems.at[6]).start()

    wait(w_o, sems.at[4])

    def out_block(c, width):
        proj = lax.dot_general(
            attn[...], w_o[pl.ds(c, width), :], contract, preferred_element_type=jnp.float32
        )
        xf = x_ref[:, pl.ds(c, width)].astype(jnp.float32)
        gate = mod_ref[2:3, pl.ds(c, width)]
        x_out[:, pl.ds(c, width)] = (xf + gate * proj).astype(jnp.bfloat16)

    def out_body(j, _):
        out_block(pl.multiple_of(j * NT, NT), NT)
        return 0

    lax.fori_loop(0, D // NT, out_body, 0)
    out_block((D // NT) * NT, D % NT)
    if final:
        norm_rows(x_out, fmod_ref.at[0:1, :], fmod_ref.at[1:2, :], normed)
        vel_ref[...] = jnp.dot(normed[...], fw_ref[...], preferred_element_type=jnp.float32)
    wait(new_rows, sems.at[6])


def run_layer(scalars, x, mod, gain, mine, theirs, stale, text, req, last=None):
    vmem = pl.BlockSpec(memory_space=pltpu.VMEM)
    hbm = pl.BlockSpec(memory_space=pl.ANY)
    final = last is not None
    operands = [scalars, x, mod, gain, *mine, *theirs, *stale, text]
    specs = [pl.BlockSpec(memory_space=pltpu.SMEM), hbm, vmem, vmem] + [hbm] * 22
    scratch = [
        pltpu.VMEM((D, D), jnp.bfloat16),
        pltpu.VMEM((D, WIDE), jnp.bfloat16),
        pltpu.VMEM((D, WIDE), jnp.bfloat16),
        pltpu.VMEM((KEYS, D), jnp.bfloat16),
        pltpu.VMEM((ROWS, D), jnp.bfloat16),
        pltpu.VMEM((ROWS, WIDE), jnp.bfloat16),
        pltpu.VMEM((ROWS, WIDE), jnp.bfloat16),
        pltpu.VMEM((NT, NT), jnp.bfloat16),
        pltpu.VMEM((ROWS, D), jnp.bfloat16),
        pltpu.SemaphoreType.DMA((7,)),
    ]
    aliases = {}
    if final:
        fmod, fw, early, new_kv = last
        operands += [fmod, fw, early]
        specs += [vmem, vmem, hbm]
        if req:
            aliases = {len(operands): 1}
            operands.append(new_kv)
            specs.append(hbm)
        outs = (
            jax.ShapeDtypeStruct((ROWS, fw.shape[1]), jnp.float32),
            jax.ShapeDtypeStruct((2, ROWS, D), jnp.bfloat16),
        )
        out_specs = (vmem, hbm)
        scratch.append(pltpu.VMEM((ROWS, D), jnp.bfloat16))
    else:
        outs = (jax.ShapeDtypeStruct((ROWS, D), jnp.bfloat16),) * 2
        out_specs = (vmem, hbm)
    return pl.pallas_call(
        lambda *refs: layer_kernel(final, req, *refs),
        name="last_layer" if final else "first_layer",
        out_shape=outs,
        in_specs=specs,
        out_specs=out_specs,
        scratch_shapes=scratch,
        input_output_aliases=aliases,
        compiler_params=pltpu.CompilerParams(vmem_limit_bytes=56 << 20),
    )(*operands)


def on_device(
    hidden,
    text_kv,
    stale_kv,
    modulation,
    score_gain,
    qkv_weight,
    out_weight,
    final_mod,
    final_weight,
    latent,
    step_index,
):
    section = lax.axis_index("section")
    shard = lax.axis_index("shard")
    z_hi, x_at, core = shard // 8, (shard // 2) % 4, shard % 2

    qkv = qkv_weight[0]
    half_kv = qkv[:, HW:]
    half_oq = jnp.concatenate([qkv[:, :HW], out_weight[0].T], 1)
    keep = jnp.where(core == 0, half_kv, half_oq)
    got = core_flip(jnp.where(core == 0, half_oq, half_kv))
    mine_block = jnp.concatenate(
        [jnp.where(core == 0, keep, got), jnp.where(core == 0, got, keep)], 0
    )
    near_z, near_x = mine_block[:, :ZC], mine_block[:, ZC:]
    text = jnp.pad(text_kv[0], ((0, 0), (0, TXT_PAD - TXT), (0, 0)))

    before_y, after_y = y_shift(stale_kv[0], 1), y_shift(stale_kv[0], -1)
    before_x, after_x = x_shift(near_x, 1), x_shift(near_x, -1)
    opposite = z_flip(mine_block)
    far_x = x_relay(jnp.where(core == 0, after(before_x, text), after_x))
    pair_z = jnp.concatenate([near_z, after(opposite, far_x)[:, :ZC]], 0)
    before_z, after_z = x_shift(pair_z, 1), x_shift(pair_z, -1)
    two_x = after(jnp.concatenate([before_x, after_x], 0), opposite)
    opposite_two = z_flip(two_x)
    far_y = y_relay(jnp.where(core == 0, before_y, after_y))
    far_z = x_relay(jnp.where(core == 0, before_z, after_z))
    opposite_far = z_flip(after(far_x, opposite_two))
    early = (mine_block, opposite, two_x, far_x)
    their_early = tuple(core_flip(after(piece, before_z)) for piece in early)
    their_before_z = core_flip(after(before_z, opposite_two))
    their_after_z = core_flip(after(after_z, opposite_two))
    their_opposite_two = core_flip(opposite_two)
    their_far_z = core_flip(far_z)
    their_opposite_far = core_flip(opposite_far)
    mine = (*early, before_z, after_z, far_z, opposite_two, opposite_far)
    theirs = (*their_early, their_before_z, their_after_z, their_far_z,
              their_opposite_two, their_opposite_far)
    stale = (before_y, after_y, far_y)
    gain = jnp.tile(score_gain[0] * (1.0 / math.sqrt(HEAD)), WIDE // HEAD)[None, :]
    rows = [
        ((z_hi ^ slot) * 4 + (x_at + dx) % 4) * BLK for slot in range(2) for dx in (0, 3, 1, 2)
    ]
    scalars = jnp.stack([core, *rows, section]).astype(jnp.int32)

    def layer(x, r, last=None):
        return run_layer(
            scalars, x, modulation[0], gain, mine, theirs, stale, text, r, last
        )

    fresh_first, arrived = [], []
    for r in range(2):
        x_next, fresh = layer(hidden, r)
        fresh_first.append(fresh)
        arrived.append(lax.ppermute(x_next, "section", [(0, 1)]))
    velocity, new_kv = [], None
    for r in range(2):
        vel, new_kv = layer(arrived[r], r, (final_mod, final_weight, fresh_first[r], new_kv))
        velocity.append(vel)
    velocity = jnp.stack(velocity)
    half = latent.shape[1]
    sent = lax.ppermute(velocity[:, :half].astype(jnp.bfloat16), "section", [(1, 0)])
    velocity_mine = jnp.where(section == 0, sent.astype(jnp.float32), velocity[:, half:])
    sig = sigma_of(step_index)[:, None, None]
    sig_next = sigma_of(step_index + 1)[:, None, None]
    latent_next = latent + (sig_next - sig) * velocity_mine
    denoised = latent - sig * velocity_mine
    return (new_kv[None], latent_next, denoised)


def solution(mesh):
    in_specs = (
        P("shard", "patch", None),
        P("section", "shard", None, None),
        P("section", "shard", "patch", None),
        P("section", "shard", None, None),
        P("section", None),
        P("section", "shard", None),
        P("section", None, "shard"),
        P("shard", None, None),
        P(),
        P("shard", ("patch", "section"), None),
        P("shard"),
    )
    out_specs = (
        P("section", "shard", "patch", None),
        P("shard", ("patch", "section"), None),
        P("shard", ("patch", "section"), None),
    )
    return jax.shard_map(
        on_device, mesh=mesh, in_specs=in_specs, out_specs=out_specs, check_vma=False
    )
```

profile of v0, /device:TPU:0, one launch (start us, length us, event | category | flops | bytes accessed | tf_op | source)
XLA Modules:
  0.0 249.4 jit_solution(16668005041717438035)
XLA Ops:
  0.7 1.1 slice.30
  1.8 1.8 broadcast_select_fusion.5
  3.6 0.1 collective-permute-start
  3.7 1.7 collective-permute-start.19
  5.5 1.6 collective-permute-start.20
  7.1 0.8 broadcast_select_fusion.4
  7.9 1.6 collective-permute-start.2
  9.6 1.7 collective-permute-start.3
  11.2 1.2 pad_maximum_fusion.refs_4_
  12.4 4.0 %collective-permute-start.1 = (bf16[304,2432]{1,0:T(8,128)(2,1)}, bf16[304,2432]{1,0:T(8,128)(2,1)S(1)}, u32[]{:S(2)}, u32[]{:S(2)}) collective-permute-start(bf16[304,2432]{1,0:T(8,128)(2,1)} %pad_maximum_fusion.refs_4_), channel_id=1, source_target_pairs={{0,8},{1,9},{2,10},{3,11},{4,12},{5,13},{6,14},{7,15},{8,0},{9,1},... | collective-permute-start | bytes 4435976 | tf_op jit(solution)/shard_map/ppermute | solution.py:54
  16.4 0.2 copy.25
  16.6 1.3 pad.4.refs_25_
  17.8 10.6 %collective-permute-done.2 = bf16[304,1280]{1,0:T(8,128)(2,1)S(1)} collective-permute-done((bf16[304,1280]{1,0:T(8,128)(2,1)S(1)}, bf16[304,1280]{1,0:T(8,128)(2,1)S(1)}, u32[]{:S(2)}, u32[]{:S(2)}) %collective-permute-start.2) | collective-permute-done | bytes 778272 | tf_op jit(solution)/shard_map/ppermute | solution.py:50
  28.5 0.1 broadcast_select_fusion.2
  28.6 1.6 collective-permute-start.4
  30.1 0.1 fusion.1
  30.2 1.3 pad_maximum_fusion.1.refs_6_
  31.5 17.0 %collective-permute-done.1.refs_5_ = bf16[304,2432]{1,0:T(8,128)(2,1)S(1)} collective-permute-done((bf16[304,2432]{1,0:T(8,128)(2,1)}, bf16[304,2432]{1,0:T(8,128)(2,1)S(1)}, u32[]{:S(2)}, u32[]{:S(2)}) %collective-permute-start.1) | collective-permute-done | bytes 1478688 | tf_op jit(solution)/shard_map/ppermute | solution.py:54
  48.5 3.2 %collective-permute-start.8 = (bf16[608,1280]{1,0:T(8,128)(2,1)}, bf16[608,1280]{1,0:T(8,128)(2,1)}, u32[]{:S(2)}, u32[]{:S(2)}) collective-permute-start(bf16[608,1280]{1,0:T(8,128)(2,1)} %pad_maximum_fusion.1.refs_6_), channel_id=1, source_target_pairs={{0,8},{1,9},{2,10},{3,11},{4,12},{5,13},{6,14},{7,15},{8,0},{9,1},... | collective-permute-start | bytes 4669448 | tf_op jit(solution)/shard_map/ppermute | solution.py:54
  51.8 0.1 pad_maximum_fusion.2
  51.9 0.3 collective-permute-start.5
  52.3 3.0 %collective-permute-start.6 = (bf16[608,1152]{1,0:T(8,128)(2,1)S(1)}, bf16[608,1152]{1,0:T(8,128)(2,1)S(1)}, u32[]{:S(2)}, u32[]{:S(2)}) collective-permute-start(bf16[608,1152]{1,0:T(8,128)(2,1)S(1)} %pad_maximum_fusion.2), channel_id=1, source_target_pairs={{0,6},{1,7},{2,0},{3,1},{4,2},{5,3},{6,4},{7,5},{8,14},{9,15},{10,... | collective-permute-start | bytes 4202504 | tf_op jit(solution)/shard_map/ppermute | solution.py:50
  55.2 6.5 %collective-permute-done.19.refs_22_ = bf16[2,256,2432]{2,1,0:T(8,128)(2,1)S(1)} collective-permute-done((bf16[2,256,2432]{2,1,0:T(8,128)(2,1)}, bf16[2,256,2432]{2,1,0:T(8,128)(2,1)S(1)}, u32[]{:S(2)}, u32[]{:S(2)}) %collective-permute-start.19) | collective-permute-done | bytes 2490400 | tf_op jit(solution)/shard_map/ppermute | solution.py:62
  61.8 0.3 broadcast_select_fusion
  62.1 1.1 copy-done
  63.2 0.8 copy-done.1
  64.0 0.9 collective-permute-start.21
  64.9 19.1 %collective-permute-done.5.refs_8_ = bf16[608,1152]{1,0:T(8,128)(2,1)S(1)} collective-permute-done((bf16[608,1152]{1,0:T(8,128)(2,1)S(1)}, bf16[608,1152]{1,0:T(8,128)(2,1)S(1)}, u32[]{:S(2)}, u32[]{:S(2)}) %collective-permute-start.5) | collective-permute-done | bytes 1400864 | tf_op jit(solution)/shard_map/ppermute | solution.py:50
  84.0 1.0 collective-permute-done.8.refs_11_
  85.0 2.9 %collective-permute-start.9 = (bf16[304,1280]{1,0:T(8,128)(2,1)S(1)}, bf16[304,1280]{1,0:T(8,128)(2,1)}, u32[]{:S(2)}, u32[]{:S(2)}) collective-permute-start(bf16[304,1280]{1,0:T(8,128)(2,1)S(1)} %collective-permute-done.4.refs_7_), channel_id=1, source_target_pairs={{0,8},{1,9},{2,10},{3,11},{4,12},{5,13},{6,14},{7,15},{8,0},{9,1},... | collective-permute-start | bytes 2334728 | tf_op jit(solution)/shard_map/ppermute | solution.py:54
  88.0 0.2 broadcast_select_fusion.1
  88.2 0.3 collective-permute-start.7
  88.5 0.6 copy-done.3
  89.1 0.6 collective-permute-start.14
  89.7 15.7 %collective-permute-done.9.refs_12_ = bf16[304,1280]{1,0:T(8,128)(2,1)} collective-permute-done((bf16[304,1280]{1,0:T(8,128)(2,1)S(1)}, bf16[304,1280]{1,0:T(8,128)(2,1)}, u32[]{:S(2)}, u32[]{:S(2)}) %collective-permute-start.9) | collective-permute-done | bytes 778272 | tf_op jit(solution)/shard_map/ppermute | solution.py:54
  105.4 0.5 collective-permute-start.12
  105.9 2.2 collective-permute-done.7.refs_10_
  108.1 0.5 collective-permute-start.10
  108.6 0.1 collective-permute-start.16
  108.7 1.2 collective-permute-done.11.refs_14_
  109.9 1.1 copy-done.7
  111.0 0.3 collective-permute-start.18
  111.3 0.6 copy.26
  112.0 0.7 broadcast_in_dim_tile.3.refs_3_
  112.6 0.7 stack.52.refs_0_
  113.3 1.8 collective-permute-done.10.refs_13_
  115.1 3.6 %collective-permute-done.18.refs_21_ = bf16[304,1280]{1,0:T(8,128)(2,1)} collective-permute-done((bf16[304,1280]{1,0:T(8,128)(2,1)}, bf16[304,1280]{1,0:T(8,128)(2,1)}, u32[]{:S(2)}, u32[]{:S(2)}) %collective-permute-start.18) | collective-permute-done | bytes 778272 | tf_op jit(solution)/shard_map/ppermute | solution.py:58
  118.7 1.2 copy-done.6
  119.9 26.8 %first_layer.3 = (bf16[256,2432]{1,0:T(8,128)(2,1)}, bf16[256,2432]{1,0:T(8,128)(2,1)}) custom-call(s32[10]{0:T(128)} %stack.52.refs_0_, bf16[2,256,2432]{2,1,0:T(8,128)(2,1)} %refs_1_.3, f32[2,3,2432]{2,1,0:T(4,128)} %bitcast.31, f32[1,1280]{1,0:T(1,128)} %broadcast_in_dim_tile.3.refs_3_, bf16[304,2432]{1,0:T(8,128)(2,1)} %pad_maximum_fusion.refs_4_, ...), custom_call_target="tpu_custom_call" | custom-call | tf_op jit(solution)/shard_map/first_layer/pallas_call | solution.py:358
  146.7 3.1 %collective-permute-start.23 = (bf16[256,2432]{1,0:T(8,128)(2,1)}, bf16[256,2432]{1,0:T(8,128)(2,1)S(1)}, u32[]{:S(2)}, u32[]{:S(2)}) collective-permute-start(bf16[256,2432]{1,0:T(8,128)(2,1)} %get-tuple-element.33), channel_id=1, source_target_pairs={{0,64},{1,65},{2,66},{3,67},{4,68},{5,69},{6,70},{7,71},{8,72},{9,... | collective-permute-start | bytes 3735560 | tf_op jit(solution)/shard_map/ppermute | solution.py:435
  149.8 26.6 %first_layer.2 = (bf16[256,2432]{1,0:T(8,128)(2,1)}, bf16[256,2432]{1,0:T(8,128)(2,1)}) custom-call(s32[10]{0:T(128)} %stack.52.refs_0_, bf16[2,256,2432]{2,1,0:T(8,128)(2,1)} %refs_1_.3, f32[2,3,2432]{2,1,0:T(4,128)} %bitcast.32, f32[1,1280]{1,0:T(1,128)} %broadcast_in_dim_tile.3.refs_3_, bf16[304,2432]{1,0:T(8,128)(2,1)} %pad_maximum_fusion.refs_4_, ...), custom_call_target="tpu_custom_call" | custom-call | tf_op jit(solution)/shard_map/first_layer/pallas_call | solution.py:358
  176.5 1.6 collective-permute-start.22
  178.1 1.1 copy.18.refs_27_
  179.1 1.0 copy-done.16
  180.2 29.2 %last_layer.2 = (f32[256,64]{1,0:T(8,128)}, bf16[2,256,2432]{2,1,0:T(8,128)(2,1)}) custom-call(s32[10]{0:T(128)} %stack.52.refs_0_, bf16[256,2432]{1,0:T(8,128)(2,1)} %copy-done.16, f32[2,3,2432]{2,1,0:T(4,128)} %bitcast.33, f32[1,1280]{1,0:T(1,128)} %broadcast_in_dim_tile.3.refs_3_, bf16[304,2432]{1,0:T(8,128)(2,1)} %pad_maximum_fusion.refs_4_, ...), custom_call_target="tpu_custom_call" | custom-call | tf_op jit(solution)/shard_map/last_layer/pallas_call | solution.py:358
  209.4 1.1 copy-done.15
  210.5 29.5 %last_layer.3 = (f32[256,64]{1,0:T(8,128)}, bf16[2,256,2432]{2,1,0:T(8,128)(2,1)}) custom-call(s32[10]{0:T(128)} %stack.52.refs_0_, bf16[256,2432]{1,0:T(8,128)(2,1)} %copy-done.15, f32[2,3,2432]{2,1,0:T(4,128)} %bitcast.34, f32[1,1280]{1,0:T(1,128)} %broadcast_in_dim_tile.3.refs_3_, ...), custom_call_target="tpu_custom_call", output_to_operand_aliasing={{1}: (29, {})} | custom-call | tf_op jit(solution)/shard_map/last_layer/pallas_call | solution.py:358
  240.0 0.9 fusion.3
  240.9 1.3 collective-permute-start.24
  242.2 0.1 copy.19
  242.3 4.7 %collective-permute-done.24 = bf16[2,128,64]{2,1,0:T(8,128)(2,1)S(1)} collective-permute-done((bf16[2,128,64]{2,1,0:T(8,128)(2,1)S(1)}, bf16[2,128,64]{2,1,0:T(8,128)(2,1)S(1)}, u32[]{:S(2)}, u32[]{:S(2)}) %collective-permute-start.24) | collective-permute-done | bytes 32800 | tf_op jit(solution)/shard_map/ppermute | solution.py:442
  247.1 0.9 multiply_subtract_fusion
  248.0 0.7 copy.21
  248.7 0.7 copy.22
  (62 shorter events, 0.3 us)
Async XLA Ops:
  0.6 6.4 %copy-start.12 = (bf16[1,152,3648]{2,1,0:T(8,128)(2,1)S(1)}, bf16[1,152,3648]{2,1,0:T(8,128)(2,1)}, u32[]{:S(2)}) copy-start(bf16[1,152,3648]{2,1,0:T(8,128)(2,1)} %param.16) | copy-start | bytes 3326980
  0.7 6.4 %copy-start.13 = (bf16[1,1216,152]{1,2,0:T(8,128)(2,1)S(1)}, bf16[1,1216,152]{1,2,0:T(8,128)(2,1)}, u32[]{:S(2)}) copy-start(bf16[1,1216,152]{1,2,0:T(8,128)(2,1)} %param.17) | copy-start | bytes 1108996
  3.6 3.4 %collective-permute-start = (bf16[152,2432]{1,0:T(8,128)(2,1)S(1)}, bf16[152,2432]{1,0:T(8,128)(2,1)S(1)}, u32[]{:S(2)}, u32[]{:S(2)}) collective-permute-start(bf16[152,2432]{1,0:T(8,128)(2,1)S(1)} %broadcast_select_fusion.5), channel_id=1, source_target_pairs={{0,1},{1,0},{2,3},{3,2},{4,5},{5,4},{6,7},{7,6},{8,9},{9,8},{10,11... | collective-permute-start | bytes 2217992 | tf_op jit(solution)/shard_map/ppermute | solution.py:58
  3.7 58.0 %collective-permute-start.19 = (bf16[2,256,2432]{2,1,0:T(8,128)(2,1)}, bf16[2,256,2432]{2,1,0:T(8,128)(2,1)S(1)}, u32[]{:S(2)}, u32[]{:S(2)}) collective-permute-start(bf16[2,256,2432]{2,1,0:T(8,128)(2,1)} %bitcast.41), channel_id=1, source_target_pairs={{0,16},{16,32},{32,48},{48,0},{1,17},{17,33},{33,49},{49,1},{2,18}... | collective-permute-start | bytes 7471112 | tf_op jit(solution)/shard_map/ppermute | solution.py:62
  5.5 56.3 %collective-permute-start.20 = (bf16[2,256,2432]{2,1,0:T(8,128)(2,1)}, bf16[2,256,2432]{2,1,0:T(8,128)(2,1)S(1)}, u32[]{:S(2)}, u32[]{:S(2)}) collective-permute-start(bf16[2,256,2432]{2,1,0:T(8,128)(2,1)} %bitcast.42), channel_id=1, source_target_pairs={{0,48},{16,0},{32,16},{48,32},{1,49},{17,1},{33,17},{49,33},{2,50}... | collective-permute-start | bytes 7471112 | tf_op jit(solution)/shard_map/ppermute | solution.py:62
  7.9 8.5 %copy-start.14 = (bf16[1,2,154,2432]{3,1,2,0:T(2,128)(2,1)S(1)}, bf16[1,2,154,2432]{3,1,2,0:T(2,128)(2,1)}, u32[]{:S(2)}) copy-start(bf16[1,2,154,2432]{3,1,2,0:T(2,128)(2,1)} %param.12) | copy-start | bytes 4494340
  7.9 20.6 %collective-permute-start.2 = (bf16[304,1280]{1,0:T(8,128)(2,1)S(1)}, bf16[304,1280]{1,0:T(8,128)(2,1)S(1)}, u32[]{:S(2)}, u32[]{:S(2)}) collective-permute-start(bf16[304,1280]{1,0:T(8,128)(2,1)S(1)} %fusion), channel_id=1, source_target_pairs={{0,2},{1,3},{2,4},{3,5},{4,6},{5,7},{6,0},{7,1},{8,10},{9,11},{10,... | collective-permute-start | bytes 2334728 | tf_op jit(solution)/shard_map/ppermute | solution.py:50
  9.6 18.9 %collective-permute-start.3 = (bf16[304,1280]{1,0:T(8,128)(2,1)S(1)}, bf16[304,1280]{1,0:T(8,128)(2,1)S(1)}, u32[]{:S(2)}, u32[]{:S(2)}) collective-permute-start(bf16[304,1280]{1,0:T(8,128)(2,1)S(1)} %fusion), channel_id=1, source_target_pairs={{0,6},{1,7},{2,0},{3,1},{4,2},{5,3},{6,4},{7,5},{8,14},{9,15},{10,... | collective-permute-start | bytes 2334728 | tf_op jit(solution)/shard_map/ppermute | solution.py:50
  12.4 36.1 %collective-permute-start.1 = (bf16[304,2432]{1,0:T(8,128)(2,1)}, bf16[304,2432]{1,0:T(8,128)(2,1)S(1)}, u32[]{:S(2)}, u32[]{:S(2)}) collective-permute-start(bf16[304,2432]{1,0:T(8,128)(2,1)} %pad_maximum_fusion.refs_4_), channel_id=1, source_target_pairs={{0,8},{1,9},{2,10},{3,11},{4,12},{5,13},{6,14},{7,15},{8,0},{9,1},... | collective-permute-start | bytes 4435976 | tf_op jit(solution)/shard_map/ppermute | solution.py:54
  28.6 23.2 %collective-permute-start.4 = (bf16[304,1280]{1,0:T(8,128)(2,1)S(1)}, bf16[304,1280]{1,0:T(8,128)(2,1)S(1)}, u32[]{:S(2)}, u32[]{:S(2)}) collective-permute-start(bf16[304,1280]{1,0:T(8,128)(2,1)S(1)} %broadcast_select_fusion.2), channel_id=1, source_target_pairs={{0,2},{1,7},{2,4},{3,1},{4,6},{5,3},{6,0},{7,5},{8,10},{9,15},{10,... | collective-permute-start | bytes 2334728 | tf_op jit(solution)/shard_map/ppermute | solution.py:72
  48.5 56.9 %copy-start.4 = (bf16[304,2432]{1,0:T(8,128)(2,1)}, bf16[304,2432]{1,0:T(8,128)(2,1)S(1)}, u32[]{:S(2)}) copy-start(bf16[304,2432]{1,0:T(8,128)(2,1)S(1)} %collective-permute-done.1.refs_5_) | copy-start | bytes 4435972
  48.5 36.5 %collective-permute-start.8 = (bf16[608,1280]{1,0:T(8,128)(2,1)}, bf16[608,1280]{1,0:T(8,128)(2,1)}, u32[]{:S(2)}, u32[]{:S(2)}) collective-permute-start(bf16[608,1280]{1,0:T(8,128)(2,1)} %pad_maximum_fusion.1.refs_6_), channel_id=1, source_target_pairs={{0,8},{1,9},{2,10},{3,11},{4,12},{5,13},{6,14},{7,15},{8,0},{9,1},... | collective-permute-start | bytes 4669448 | tf_op jit(solution)/shard_map/ppermute | solution.py:54
  51.8 33.3 %copy-start.10 = (bf16[304,1280]{1,0:T(8,128)(2,1)}, bf16[304,1280]{1,0:T(8,128)(2,1)S(1)}, u32[]{:S(2)}) copy-start(bf16[304,1280]{1,0:T(8,128)(2,1)S(1)} %collective-permute-done.4.refs_7_) | copy-start | bytes 2334724
  51.9 32.1 %collective-permute-start.5 = (bf16[608,1152]{1,0:T(8,128)(2,1)S(1)}, bf16[608,1152]{1,0:T(8,128)(2,1)S(1)}, u32[]{:S(2)}, u32[]{:S(2)}) collective-permute-start(bf16[608,1152]{1,0:T(8,128)(2,1)S(1)} %pad_maximum_fusion.2), channel_id=1, source_target_pairs={{0,2},{1,3},{2,4},{3,5},{4,6},{5,7},{6,0},{7,1},{8,10},{9,11},{10,... | collective-permute-start | bytes 4202504 | tf_op jit(solution)/shard_map/ppermute | solution.py:50
  52.3 35.7 %collective-permute-start.6 = (bf16[608,1152]{1,0:T(8,128)(2,1)S(1)}, bf16[608,1152]{1,0:T(8,128)(2,1)S(1)}, u32[]{:S(2)}, u32[]{:S(2)}) collective-permute-start(bf16[608,1152]{1,0:T(8,128)(2,1)S(1)} %pad_maximum_fusion.2), channel_id=1, source_target_pairs={{0,6},{1,7},{2,0},{3,1},{4,2},{5,3},{6,4},{7,5},{8,14},{9,15},{10,... | collective-permute-start | bytes 4202504 | tf_op jit(solution)/shard_map/ppermute | solution.py:50
  61.8 1.4 copy-start
  61.8 2.2 copy-start.1
  64.0 47.3 %copy-start.20 = (f32[1,2,3,2432]{3,1,2,0:T(2,128)S(1)}, f32[1,2,3,2432]{3,1,2,0:T(2,128)}, u32[]{:S(2)}) copy-start(f32[1,2,3,2432]{3,1,2,0:T(2,128)} %param.14) | copy-start | bytes 175108
  64.0 47.9 %copy-start.21 = (f32[1,64]{1,0:T(1,128)S(1)}, f32[1,64]{1,0:T(1,128)}, u32[]{:S(2)}) copy-start(f32[1,64]{1,0:T(1,128)} %param.15) | copy-start | bytes 772
  64.0 41.4 %collective-permute-start.21 = (bf16[2,256,2432]{2,1,0:T(8,128)(2,1)S(1)}, bf16[2,256,2432]{2,1,0:T(8,128)(2,1)}, u32[]{:S(2)}, u32[]{:S(2)}) collective-permute-start(bf16[2,256,2432]{2,1,0:T(8,128)(2,1)S(1)} %broadcast_select_fusion), channel_id=1, source_target_pairs={{0,16},{1,49},{2,18},{3,51},{4,20},{5,53},{6,22},{7,55},{8,24},{9,... | collective-permute-start | bytes 7471112 | tf_op jit(solution)/shard_map/ppermute | solution.py:81
  84.0 5.1 %copy-start.2 = (bf16[608,1152]{1,0:T(8,128)(2,1)}, bf16[608,1152]{1,0:T(8,128)(2,1)S(1)}, u32[]{:S(2)}) copy-start(bf16[608,1152]{1,0:T(8,128)(2,1)S(1)} %collective-permute-done.5.refs_8_) | copy-start | bytes 4202500
  84.0 5.1 %collective-permute-start.13 = (bf16[304,1280]{1,0:T(8,128)(2,1)S(1)}, bf16[304,1280]{1,0:T(8,128)(2,1)S(1)}, u32[]{:S(2)}, u32[]{:S(2)}) collective-permute-start(bf16[304,1280]{1,0:T(8,128)(2,1)S(1)} %collective-permute-done.4.refs_7_), channel_id=1, source_target_pairs={{0,1},{1,0},{2,3},{3,2},{4,5},{5,4},{6,7},{7,6},{8,9},{9,8},{10,11... | collective-permute-start | bytes 2334728 | tf_op jit(solution)/shard_map/ppermute | solution.py:58
  85.0 20.4 %collective-permute-start.9 = (bf16[304,1280]{1,0:T(8,128)(2,1)S(1)}, bf16[304,1280]{1,0:T(8,128)(2,1)}, u32[]{:S(2)}, u32[]{:S(2)}) collective-permute-start(bf16[304,1280]{1,0:T(8,128)(2,1)S(1)} %collective-permute-done.4.refs_7_), channel_id=1, source_target_pairs={{0,8},{1,9},{2,10},{3,11},{4,12},{5,13},{6,14},{7,15},{8,0},{9,1},... | collective-permute-start | bytes 2334728 | tf_op jit(solution)/shard_map/ppermute | solution.py:54
  88.0 1.1 copy-start.3
  88.2 20.0 %collective-permute-start.7 = (bf16[608,1152]{1,0:T(8,128)(2,1)S(1)}, bf16[608,1152]{1,0:T(8,128)(2,1)}, u32[]{:S(2)}, u32[]{:S(2)}) collective-permute-start(bf16[608,1152]{1,0:T(8,128)(2,1)S(1)} %broadcast_select_fusion.1), channel_id=1, source_target_pairs={{0,2},{1,7},{2,4},{3,1},{4,6},{5,3},{6,0},{7,5},{8,10},{9,15},{10,... | collective-permute-start | bytes 4202504 | tf_op jit(solution)/shard_map/ppermute | solution.py:72
  89.1 19.1 %collective-permute-start.15 = (bf16[608,1152]{1,0:T(8,128)(2,1)S(1)}, bf16[608,1152]{1,0:T(8,128)(2,1)S(1)}, u32[]{:S(2)}, u32[]{:S(2)}) collective-permute-start(bf16[608,1152]{1,0:T(8,128)(2,1)S(1)} %collective-permute-done.6.refs_9_), channel_id=1, source_target_pairs={{0,1},{1,0},{2,3},{3,2},{4,5},{5,4},{6,7},{7,6},{8,9},{9,8},{10,11... | collective-permute-start | bytes 4202504 | tf_op jit(solution)/shard_map/ppermute | solution.py:58
  89.1 20.8 %copy-start.11 = (bf16[304,1280]{1,0:T(8,128)(2,1)}, bf16[304,1280]{1,0:T(8,128)(2,1)S(1)}, u32[]{:S(2)}) copy-start(bf16[304,1280]{1,0:T(8,128)(2,1)S(1)} %collective-permute-done.13.refs_16_) | copy-start | bytes 2334724
  89.1 19.6 %collective-permute-start.14 = (bf16[608,1152]{1,0:T(8,128)(2,1)S(1)}, bf16[608,1152]{1,0:T(8,128)(2,1)S(1)}, u32[]{:S(2)}, u32[]{:S(2)}) collective-permute-start(bf16[608,1152]{1,0:T(8,128)(2,1)S(1)} %collective-permute-done.5.refs_8_), channel_id=1, source_target_pairs={{0,1},{1,0},{2,3},{3,2},{4,5},{5,4},{6,7},{7,6},{8,9},{9,8},{10,11... | collective-permute-start | bytes 4202504 | tf_op jit(solution)/shard_map/ppermute | solution.py:58
  105.4 4.5 %collective-permute-start.11 = (bf16[304,2432]{1,0:T(8,128)(2,1)S(1)}, bf16[304,2432]{1,0:T(8,128)(2,1)S(1)}, u32[]{:S(2)}, u32[]{:S(2)}) collective-permute-start(bf16[304,2432]{1,0:T(8,128)(2,1)S(1)} %collective-permute-done.1.refs_5_), channel_id=1, source_target_pairs={{0,1},{1,0},{2,3},{3,2},{4,5},{5,4},{6,7},{7,6},{8,9},{9,8},{10,11... | collective-permute-start | bytes 4435976 | tf_op jit(solution)/shard_map/ppermute | solution.py:58
  105.4 9.7 %collective-permute-start.12 = (bf16[608,1280]{1,0:T(8,128)(2,1)}, bf16[608,1280]{1,0:T(8,128)(2,1)S(1)}, u32[]{:S(2)}, u32[]{:S(2)}) collective-permute-start(bf16[608,1280]{1,0:T(8,128)(2,1)} %pad_maximum_fusion.1.refs_6_), channel_id=1, source_target_pairs={{0,1},{1,0},{2,3},{3,2},{4,5},{5,4},{6,7},{7,6},{8,9},{9,8},{10,11... | collective-permute-start | bytes 4669448 | tf_op jit(solution)/shard_map/ppermute | solution.py:58
  108.1 10.6 %collective-permute-start.17 = (bf16[608,1280]{1,0:T(8,128)(2,1)}, bf16[608,1280]{1,0:T(8,128)(2,1)S(1)}, u32[]{:S(2)}, u32[]{:S(2)}) collective-permute-start(bf16[608,1280]{1,0:T(8,128)(2,1)} %collective-permute-done.8.refs_11_), channel_id=1, source_target_pairs={{0,1},{1,0},{2,3},{3,2},{4,5},{5,4},{6,7},{7,6},{8,9},{9,8},{10,11... | collective-permute-start | bytes 4669448 | tf_op jit(solution)/shard_map/ppermute | solution.py:58
  108.1 1.8 copy-start.8
  108.1 7.0 %collective-permute-start.10 = (bf16[304,2432]{1,0:T(8,128)(2,1)}, bf16[304,2432]{1,0:T(8,128)(2,1)}, u32[]{:S(2)}, u32[]{:S(2)}) collective-permute-start(bf16[304,2432]{1,0:T(8,128)(2,1)} %pad_maximum_fusion.refs_4_), channel_id=1, source_target_pairs={{0,1},{1,0},{2,3},{3,2},{4,5},{5,4},{6,7},{7,6},{8,9},{9,8},{10,11... | collective-permute-start | bytes 4435976 | tf_op jit(solution)/shard_map/ppermute | solution.py:58
  108.6 1.3 copy-start.9
  108.6 10.1 %collective-permute-start.16 = (bf16[608,1152]{1,0:T(8,128)(2,1)}, bf16[608,1152]{1,0:T(8,128)(2,1)}, u32[]{:S(2)}, u32[]{:S(2)}) collective-permute-start(bf16[608,1152]{1,0:T(8,128)(2,1)} %collective-permute-done.7.refs_10_), channel_id=1, source_target_pairs={{0,1},{1,0},{2,3},{3,2},{4,5},{5,4},{6,7},{7,6},{8,9},{9,8},{10,11... | collective-permute-start | bytes 4202504 | tf_op jit(solution)/shard_map/ppermute | solution.py:58
  109.9 1.1 copy-start.7
  111.0 7.7 %collective-permute-start.18 = (bf16[304,1280]{1,0:T(8,128)(2,1)}, bf16[304,1280]{1,0:T(8,128)(2,1)}, u32[]{:S(2)}, u32[]{:S(2)}) collective-permute-start(bf16[304,1280]{1,0:T(8,128)(2,1)} %collective-permute-done.9.refs_12_), channel_id=1, source_target_pairs={{0,1},{1,0},{2,3},{3,2},{4,5},{5,4},{6,7},{7,6},{8,9},{9,8},{10,11... | collective-permute-start | bytes 2334728 | tf_op jit(solution)/shard_map/ppermute | solution.py:58
  115.1 3.6 %copy-start.5 = (bf16[608,1280]{1,0:T(8,128)(2,1)}, bf16[608,1280]{1,0:T(8,128)(2,1)S(1)}, u32[]{:S(2)}) copy-start(bf16[608,1280]{1,0:T(8,128)(2,1)S(1)} %collective-permute-done.12.refs_15_) | copy-start | bytes 4669444
  118.7 1.2 copy-start.6
  146.7 31.4 %copy-start.18 = (bf16[2432,64]{0,1:T(8,128)(2,1)S(1)}, bf16[2432,64]{0,1:T(8,128)(2,1)}, u32[]{:S(2)}) copy-start(bf16[2432,64]{0,1:T(8,128)(2,1)} %param.19) | copy-start | bytes 933892
  146.7 32.5 %collective-permute-start.23 = (bf16[256,2432]{1,0:T(8,128)(2,1)}, bf16[256,2432]{1,0:T(8,128)(2,1)S(1)}, u32[]{:S(2)}, u32[]{:S(2)}) collective-permute-start(bf16[256,2432]{1,0:T(8,128)(2,1)} %get-tuple-element.33), channel_id=1, source_target_pairs={{0,64},{1,65},{2,66},{3,67},{4,68},{5,69},{6,70},{7,71},{8,72},{9,... | collective-permute-start | bytes 3735560 | tf_op jit(solution)/shard_map/ppermute | solution.py:435
  176.5 33.0 %collective-permute-start.22 = (bf16[256,2432]{1,0:T(8,128)(2,1)}, bf16[256,2432]{1,0:T(8,128)(2,1)S(1)}, u32[]{:S(2)}, u32[]{:S(2)}) collective-permute-start(bf16[256,2432]{1,0:T(8,128)(2,1)} %get-tuple-element.31), channel_id=1, source_target_pairs={{0,64},{1,65},{2,66},{3,67},{4,68},{5,69},{6,70},{7,71},{8,72},{9,... | collective-permute-start | bytes 3735560 | tf_op jit(solution)/shard_map/ppermute | solution.py:435
  179.1 1.0 copy-start.16
  209.4 1.1 copy-start.15
  210.5 29.5 %copy-start.17 = (f32[256,64]{1,0:T(8,128)S(1)}, f32[256,64]{1,0:T(8,128)}, u32[]{:S(2)}) copy-start(f32[256,64]{1,0:T(8,128)} %get-tuple-element.37) | copy-start | bytes 196612
  210.5 31.7 %copy-start.22 = (s32[2]{0:T(128)S(1)}, s32[2]{0:T(128)}, u32[]{:S(2)}) copy-start(s32[2]{0:T(128)} %param.21) | copy-start | bytes 28
  210.5 31.7 %copy-start.19 = (f32[2,128,64]{1,2,0:T(8,128)S(1)}, f32[2,128,64]{1,2,0:T(8,128)}, u32[]{:S(2)}) copy-start(f32[2,128,64]{1,2,0:T(8,128)} %param.20) | copy-start | bytes 196612
  240.9 6.2 %collective-permute-start.24 = (bf16[2,128,64]{2,1,0:T(8,128)(2,1)S(1)}, bf16[2,128,64]{2,1,0:T(8,128)(2,1)S(1)}, u32[]{:S(2)}, u32[]{:S(2)}) collective-permute-start(bf16[2,128,64]{2,1,0:T(8,128)(2,1)S(1)} %fusion.3), channel_id=1, source_target_pairs={{64,0},{65,1},{66,2},{67,3},{68,4},{69,5},{70,6},{71,7},{72,8},{73... | collective-permute-start | bytes 98312 | tf_op jit(solution)/shard_map/ppermute | solution.py:442
where the time goes:
time: 250 us; the launch traced here: 249 us
  Pallas kernels  112 us (45%)
  waiting for transfers between devices  83.5 us (33%)
  starting transfers between devices  30.9 us (12%)
  local copies, waits for them, and re-layouts  14.1 us (6%)
  other arithmetic  7.75 us (3%)
    pallas_call x4, Pallas kernels, run_layer(): pl.pallas_call(lambda *refs: layer_kernel(final, req, *refs), name='last_...  112 us
    ppermute x3, waiting for transfers between devices, z_flip(): return lax.ppermute(value, 'shard', shard_pairs(flip_z=1))  33.7 us
    ppermute x4, waiting for transfers between devices, x_shift(): return lax.ppermute(value, 'shard', shard_pairs(dx=dx))  29.8 us
    unnamed x52, local copies, waits for them, and re-layouts  10.3 us
    ppermute x3, starting transfers between devices, z_flip(): return lax.ppermute(value, 'shard', shard_pairs(flip_z=1))  10.1 us
    ppermute x4, starting transfers between devices, x_shift(): return lax.ppermute(value, 'shard', shard_pairs(dx=dx))  6.61 us
    ppermute x2, waiting for transfers between devices, y_shift(): return lax.ppermute(value, 'patch', ring_pairs(dy))  6.55 us
    ppermute x10, waiting for transfers between devices, core_flip(): return lax.ppermute(value, 'shard', shard_pairs(flip_core=1))  6.55 us
  transfers between devices with their start and end apart: 25, of which 11 were waited for; matrix products, arithmetic and copies ran while one was open for 4% of the time, Pallas kernels for 22%

commit v1 on v0

--- a/solution.py
+++ b/solution.py
@@ -16,7 +16,7 @@
 TXT_PAD = 160
 KEYS = 4 * ROWS + TXT_PAD
 BLK = 304
-ZC = 1152
+ZC = 1408
 XC = D - ZC
 WIDE = 1280
 LANE = 128
@@ -119,9 +119,9 @@
     if final:
         fmod_ref, fw_ref, early_ref = refs[0].at[req], refs[1], refs[2]
         refs = refs[4:] if req else refs[3:]
-        vel_ref, fresh_ref = refs[:2]
+        low_ref, fresh_ref, high_ref = refs[:3]
         fresh_ref = fresh_ref.at[req]
-        w_kv, w_q, w_o, kv, normed, qbuf, attn, ones, x_ref, sems, x_out = refs[2:]
+        w_kv, w_q, w_o, kv, normed, qbuf, attn, ones, x_ref, sems, x_out = refs[3:]
     else:
         x_hbm = x_hbm.at[req]
         x_out, fresh_ref = refs[:2]
@@ -135,20 +135,19 @@
             sem,
         ).start()
 
-    def spread_z(pieces, dst, sem):
-        put(pieces[0], 0, 0, ZC, dst, 0, 0, 0, sem)
-        put(pieces[1], 0, 0, ZC, dst, 1, 0, 0, sem)
+    def spread_z(pieces, col, count, dst, dst_col, sem):
+        put(pieces[0], 0, col, count, dst, 0, 0, dst_col, sem)
+        put(pieces[1], 0, col, count, dst, 1, 0, dst_col, sem)
         for j, ref in enumerate(pieces[4:7]):
             for slot in range(2):
-                put(ref, slot * BLK, 0, ZC, dst, slot, j + 1, 0, sem)
-
-    def spread_x(pieces, count, dst, dst_col, sem):
+                put(ref, slot * BLK, col, count, dst, slot, j + 1, dst_col, sem)
+
+    def spread_x(pieces, dst, dst_col, sem):
         for slot in range(2):
-            near, two, far = pieces[slot], pieces[(2, 7)[slot]], pieces[(3, 8)[slot]]
-            put(near, 0, ZC, count, dst, slot, 0, dst_col, sem)
-            for j in range(2):
-                put(two, j * BLK, 0, count, dst, slot, j + 1, dst_col, sem)
-            put(far, 0, 0, count, dst, slot, 3, dst_col, sem)
+            three, far = pieces[(2, 7)[slot]], pieces[(3, 8)[slot]]
+            for j in range(3):
+                put(three, j * BLK, 0, XC, dst, slot, j, dst_col, sem)
+            put(far, 0, 0, XC, dst, slot, 3, dst_col, sem)
 
     def by_core(step):
         @pl.when(sc[0] == 0)
@@ -160,17 +159,17 @@
             step(theirs, mine)
 
     def fetch_kv_z(kv_pieces, oq_pieces):
-        spread_z(kv_pieces, w_kv, sems.at[0])
+        spread_z(kv_pieces, 0, ZC, w_kv, 0, sems.at[0])
 
     def fetch_kv_x(kv_pieces, oq_pieces):
-        spread_x(kv_pieces, XC, w_kv, ZC, sems.at[1])
+        spread_x(kv_pieces, w_kv, ZC, sems.at[1])
 
     def fetch_q(kv_pieces, oq_pieces):
-        spread_z(oq_pieces, w_q, sems.at[2])
-        spread_x(oq_pieces, WIDE - ZC, w_q, ZC, sems.at[2])
+        spread_z(oq_pieces, 0, WIDE, w_q, 0, sems.at[2])
 
     def fetch_out(kv_pieces, oq_pieces):
-        spread_x(oq_pieces, XC, w_o, 0, sems.at[4])
+        spread_z(oq_pieces, D - WIDE, ZC + WIDE - D, w_o, 0, sems.at[4])
+        spread_x(oq_pieces, w_o, ZC + WIDE - D, sems.at[4])
 
     def fetch_keys():
         for j, ref in enumerate((*stale, text_ref)):
@@ -203,10 +202,9 @@
         kv[pl.ds(0, ROWS), pl.ds(c, NT)] = out.astype(jnp.bfloat16)
         return 0
 
-    lax.fori_loop(0, ZC // NT, key_block, 0)
+    lax.fori_loop(0, WIDE // NT, key_block, 0)
     wait(w_kv.at[:, pl.ds(ZC, XC)], sems.at[1])
     fetch_keys()
-    key_block(ZC // NT, 0)
     vw = 384
 
     def value_block(j, _):
@@ -315,7 +313,10 @@
     out_block((D // NT) * NT, D % NT)
     if final:
         norm_rows(x_out, fmod_ref.at[0:1, :], fmod_ref.at[1:2, :], normed)
-        vel_ref[...] = jnp.dot(normed[...], fw_ref[...], preferred_element_type=jnp.float32)
+        vel = jnp.dot(normed[...], fw_ref[...], preferred_element_type=jnp.float32)
+        half = ROWS // 2
+        low_ref[...] = vel[:half].astype(jnp.bfloat16)
+        high_ref[...] = vel[half:]
     wait(new_rows, sems.at[6])
 
 
@@ -347,10 +348,11 @@
             operands.append(new_kv)
             specs.append(hbm)
         outs = (
-            jax.ShapeDtypeStruct((ROWS, fw.shape[1]), jnp.float32),
+            jax.ShapeDtypeStruct((ROWS // 2, fw.shape[1]), jnp.bfloat16),
             jax.ShapeDtypeStruct((2, ROWS, D), jnp.bfloat16),
+            jax.ShapeDtypeStruct((ROWS // 2, fw.shape[1]), jnp.float32),
         )
-        out_specs = (vmem, hbm)
+        out_specs = (vmem, hbm, vmem)
         scratch.append(pltpu.VMEM((ROWS, D), jnp.bfloat16))
     else:
         outs = (jax.ShapeDtypeStruct((ROWS, D), jnp.bfloat16),) * 2
@@ -395,27 +397,27 @@
     near_z, near_x = mine_block[:, :ZC], mine_block[:, ZC:]
     text = jnp.pad(text_kv[0], ((0, 0), (0, TXT_PAD - TXT), (0, 0)))
 
+    before_x, after_x = x_shift(near_x, 1), x_shift(near_x, -1)
+    opposite_z = z_flip(near_z)
     before_y, after_y = y_shift(stale_kv[0], 1), y_shift(stale_kv[0], -1)
-    before_x, after_x = x_shift(near_x, 1), x_shift(near_x, -1)
-    opposite = z_flip(mine_block)
     far_x = x_relay(jnp.where(core == 0, after(before_x, text), after_x))
-    pair_z = jnp.concatenate([near_z, after(opposite, far_x)[:, :ZC]], 0)
+    three_x = jnp.concatenate([near_x, before_x, after_x], 0)
+    opposite_three = z_flip(three_x)
+    pair_z = jnp.concatenate([near_z, opposite_z], 0)
     before_z, after_z = x_shift(pair_z, 1), x_shift(pair_z, -1)
-    two_x = after(jnp.concatenate([before_x, after_x], 0), opposite)
-    opposite_two = z_flip(two_x)
-    far_y = y_relay(jnp.where(core == 0, before_y, after_y))
+    far_y = y_relay(jnp.where(core == 0, after(before_y, far_x), after_y))
     far_z = x_relay(jnp.where(core == 0, before_z, after_z))
-    opposite_far = z_flip(after(far_x, opposite_two))
-    early = (mine_block, opposite, two_x, far_x)
+    opposite_far = z_flip(after(far_x, opposite_three))
+    early = (near_z, opposite_z, three_x, far_x)
     their_early = tuple(core_flip(after(piece, before_z)) for piece in early)
-    their_before_z = core_flip(after(before_z, opposite_two))
-    their_after_z = core_flip(after(after_z, opposite_two))
-    their_opposite_two = core_flip(opposite_two)
-    their_far_z = core_flip(far_z)
-    their_opposite_far = core_flip(opposite_far)
-    mine = (*early, before_z, after_z, far_z, opposite_two, opposite_far)
+    their_before_z = core_flip(after(before_z, far_y))
+    their_after_z = core_flip(after(after_z, far_y))
+    their_far_z = core_flip(after(far_z, far_y))
+    their_opposite_three = core_flip(after(opposite_three, far_y))
+    their_opposite_far = core_flip(after(opposite_far, far_y))
+    mine = (*early, before_z, after_z, far_z, opposite_three, opposite_far)
     theirs = (*their_early, their_before_z, their_after_z, their_far_z,
-              their_opposite_two, their_opposite_far)
+              their_opposite_three, their_opposite_far)
     stale = (before_y, after_y, far_y)
     gain = jnp.tile(score_gain[0] * (1.0 / math.sqrt(HEAD)), WIDE // HEAD)[None, :]
     rows = [
@@ -435,12 +437,10 @@
         arrived.append(lax.ppermute(x_next, "section", [(0, 1)]))
     velocity, new_kv = [], None
     for r in range(2):
-        vel, new_kv = layer(arrived[r], r, (final_mod, final_weight, fresh_first[r], new_kv))
-        velocity.append(vel)
-    velocity = jnp.stack(velocity)
-    half = latent.shape[1]
-    sent = lax.ppermute(velocity[:, :half].astype(jnp.bfloat16), "section", [(1, 0)])
-    velocity_mine = jnp.where(section == 0, sent.astype(jnp.float32), velocity[:, half:])
+        low, new_kv, high = layer(arrived[r], r, (final_mod, final_weight, fresh_first[r], new_kv))
+        sent = lax.ppermute(low, "section", [(1, 0)])
+        velocity.append(jnp.where(section == 0, sent.astype(jnp.float32), high))
+    velocity_mine = jnp.stack(velocity)
     sig = sigma_of(step_index)[:, None, None]
     sig_next = sigma_of(step_index + 1)[:, None, None]
     latent_next = latent + (sig_next - sig) * velocity_mine

time: 250 us -> 241 us (0.964)
  waiting for transfers between devices: 83.5 us -> 77 us
  other arithmetic: 7.75 us -> 5.12 us
    ppermute x2, waiting for transfers between devices: 6.55 us -> 20.2 us  [y_shift(): return lax.ppermute(value, 'patch', ring_pairs(dy))]
    ppermute x4, waiting for transfers between devices: 29.8 us -> 17 us  [x_shift(): return lax.ppermute(value, 'shard', shard_pairs(dx=dx))]
    ppermute x3, waiting for transfers between devices: 33.7 us -> 22.5 us  [z_flip(): return lax.ppermute(value, 'shard', shard_pairs(flip_z=1))]
    unnamed x52 -> x54, local copies, waits for them, and re-layouts: 10.3 us -> 8.68 us
  transfers between devices with their start and end apart: 25 -> 26, of which waited for: 11 -> 14; matrix products, arithmetic and copies ran while one was open for 4% -> 3% of each run, Pallas kernels for 22% -> 35%
where the time goes in v1:
time: 241 us
  Pallas kernels  112 us (46%)
  waiting for transfers between devices  77 us (32%)
  starting transfers between devices  33.2 us (14%)
  local copies, waits for them, and re-layouts  12.4 us (5%)
  other arithmetic  5.12 us (2%)
    pallas_call x4, Pallas kernels, run_layer(): pl.pallas_call(lambda *refs: layer_kernel(final, req, *refs), name='last_...  112 us
    ppermute x3, waiting for transfers between devices, z_flip(): return lax.ppermute(value, 'shard', shard_pairs(flip_z=1))  22.5 us
    ppermute x2, waiting for transfers between devices, y_shift(): return lax.ppermute(value, 'patch', ring_pairs(dy))  20.2 us
    ppermute x4, waiting for transfers between devices, x_shift(): return lax.ppermute(value, 'shard', shard_pairs(dx=dx))  17 us
    ppermute x3, starting transfers between devices, z_flip(): return lax.ppermute(value, 'shard', shard_pairs(flip_z=1))  11 us
    unnamed x54, local copies, waits for them, and re-layouts  8.68 us
    ppermute x10, waiting for transfers between devices, core_flip(): return lax.ppermute(value, 'shard', shard_pairs(flip_core=1))  8.38 us
    ppermute x4, starting transfers between devices, x_shift(): return lax.ppermute(value, 'shard', shard_pairs(dx=dx))  6.61 us
  transfers between devices with their start and end apart: 26, of which 14 were waited for; matrix products, arithmetic and copies ran while one was open for 3% of the time, Pallas kernels for 35%

profile of v1, /device:TPU:0, one launch (start us, length us, event | category | flops | bytes accessed | tf_op | source)
XLA Modules:
  0.0 240.8 jit_solution(14514579151609065798)
XLA Ops:
  0.7 1.1 slice.17
  1.8 1.8 broadcast_select_fusion.4
  3.6 0.1 collective-permute-start
  3.7 1.7 collective-permute-start.14
  5.5 1.6 collective-permute-start.15
  7.0 0.8 broadcast_select_fusion.2
  7.9 1.6 collective-permute-start.2
  9.6 1.7 collective-permute-start.3
  11.3 4.0 %collective-permute-start.1 = (bf16[304,1408]{1,0:T(8,128)(2,1)S(1)}, bf16[304,1408]{1,0:T(8,128)(2,1)S(1)}, u32[]{:S(2)}, u32[]{:S(2)}) collective-permute-start(bf16[304,1408]{1,0:T(8,128)(2,1)S(1)} %fusion.refs_4_), channel_id=1, source_target_pairs={{0,8},{1,9},{2,10},{3,11},{4,12},{5,13},{6,14},{7,15},{8,0},{9,1},... | collective-permute-start | bytes 2568200 | tf_op jit(solution)/shard_map/ppermute | solution.py:54
  15.3 0.2 copy.25
  15.5 1.3 pad.4.refs_25_
  16.8 8.4 %collective-permute-done.2 = bf16[304,1024]{1,0:T(8,128)(2,1)S(1)} collective-permute-done((bf16[304,1024]{1,0:T(8,128)(2,1)S(1)}, bf16[304,1024]{1,0:T(8,128)(2,1)S(1)}, u32[]{:S(2)}, u32[]{:S(2)}) %collective-permute-start.2) | collective-permute-done | bytes 622624 | tf_op jit(solution)/shard_map/ppermute | solution.py:50
  25.2 1.6 collective-permute-start.4
  26.8 7.1 %collective-permute-done.1.refs_5_ = bf16[304,1408]{1,0:T(8,128)(2,1)S(1)} collective-permute-done((bf16[304,1408]{1,0:T(8,128)(2,1)S(1)}, bf16[304,1408]{1,0:T(8,128)(2,1)S(1)}, u32[]{:S(2)}, u32[]{:S(2)}) %collective-permute-start.1) | collective-permute-done | bytes 856096 | tf_op jit(solution)/shard_map/ppermute | solution.py:54
  33.9 0.1 pad_maximum_fusion.1
  34.0 0.3 collective-permute-start.5
  34.4 3.0 %collective-permute-start.6 = (bf16[608,1408]{1,0:T(8,128)(2,1)S(1)}, bf16[608,1408]{1,0:T(8,128)(2,1)}, u32[]{:S(2)}, u32[]{:S(2)}) collective-permute-start(bf16[608,1408]{1,0:T(8,128)(2,1)S(1)} %pad_maximum_fusion.1), channel_id=1, source_target_pairs={{0,6},{1,7},{2,0},{3,1},{4,2},{5,3},{6,4},{7,5},{8,14},{9,15},{10,... | collective-permute-start | bytes 5136392 | tf_op jit(solution)/shard_map/ppermute | solution.py:50
  37.3 0.1 pad_maximum_fusion.refs_6_
  37.5 4.0 %collective-permute-start.8 = (bf16[912,1024]{1,0:T(8,128)(2,1)S(1)}, bf16[912,1024]{1,0:T(8,128)(2,1)}, u32[]{:S(2)}, u32[]{:S(2)}) collective-permute-start(bf16[912,1024]{1,0:T(8,128)(2,1)S(1)} %pad_maximum_fusion.refs_6_), channel_id=1, source_target_pairs={{0,8},{1,9},{2,10},{3,11},{4,12},{5,13},{6,14},{7,15},{8,0},{9,1},... | collective-permute-start | bytes 5603336 | tf_op jit(solution)/shard_map/ppermute | solution.py:54
  41.6 20.2 %collective-permute-done.14.refs_22_ = bf16[2,256,2432]{2,1,0:T(8,128)(2,1)S(1)} collective-permute-done((bf16[2,256,2432]{2,1,0:T(8,128)(2,1)}, bf16[2,256,2432]{2,1,0:T(8,128)(2,1)S(1)}, u32[]{:S(2)}, u32[]{:S(2)}) %collective-permute-start.14) | collective-permute-done | bytes 2490400 | tf_op jit(solution)/shard_map/ppermute | solution.py:62
  61.8 0.3 broadcast_select_fusion
  62.1 1.2 copy-done
  63.2 0.8 copy-done.1
  64.0 0.9 collective-permute-start.16
  64.9 8.7 %collective-permute-done.5.refs_8_ = bf16[608,1408]{1,0:T(8,128)(2,1)} collective-permute-done((bf16[608,1408]{1,0:T(8,128)(2,1)S(1)}, bf16[608,1408]{1,0:T(8,128)(2,1)}, u32[]{:S(2)}, u32[]{:S(2)}) %collective-permute-start.5) | collective-permute-done | bytes 1712160 | tf_op jit(solution)/shard_map/ppermute | solution.py:50
  73.5 1.6 broadcast_select_fusion.1
  75.2 0.3 collective-permute-start.7
  75.5 4.5 %collective-permute-done.8.refs_11_ = bf16[912,1024]{1,0:T(8,128)(2,1)} collective-permute-done((bf16[912,1024]{1,0:T(8,128)(2,1)S(1)}, bf16[912,1024]{1,0:T(8,128)(2,1)}, u32[]{:S(2)}, u32[]{:S(2)}) %collective-permute-start.8) | collective-permute-done | bytes 1867808 | tf_op jit(solution)/shard_map/ppermute | solution.py:54
  80.0 2.9 %collective-permute-start.9 = (bf16[304,1024]{1,0:T(8,128)(2,1)S(1)}, bf16[304,1024]{1,0:T(8,128)(2,1)S(1)}, u32[]{:S(2)}, u32[]{:S(2)}) collective-permute-start(bf16[304,1024]{1,0:T(8,128)(2,1)S(1)} %collective-permute-done.4.refs_7_), channel_id=1, source_target_pairs={{0,8},{1,9},{2,10},{3,11},{4,12},{5,13},{6,14},{7,15},{8,0},{9,1},... | collective-permute-start | bytes 1867784 | tf_op jit(solution)/shard_map/ppermute | solution.py:54
  83.0 0.5 collective-permute-start.10
  83.5 10.8 %collective-permute-done.9.refs_12_ = bf16[304,1024]{1,0:T(8,128)(2,1)S(1)} collective-permute-done((bf16[304,1024]{1,0:T(8,128)(2,1)S(1)}, bf16[304,1024]{1,0:T(8,128)(2,1)S(1)}, u32[]{:S(2)}, u32[]{:S(2)}) %collective-permute-start.9) | collective-permute-done | bytes 622624 | tf_op jit(solution)/shard_map/ppermute | solution.py:54
  94.3 1.1 collective-permute-done.16.refs_24_
  95.5 3.0 %collective-permute-done.7.refs_10_ = bf16[608,1408]{1,0:T(8,128)(2,1)} collective-permute-done((bf16[608,1408]{1,0:T(8,128)(2,1)S(1)}, bf16[608,1408]{1,0:T(8,128)(2,1)}, u32[]{:S(2)}, u32[]{:S(2)}) %collective-permute-start.7) | collective-permute-done | bytes 1712160 | tf_op jit(solution)/shard_map/ppermute | solution.py:72
  98.5 0.6 collective-permute-done.13.refs_16_
  99.1 0.1 collective-permute-start.17
  99.2 0.4 collective-permute-start.18
  99.6 0.1 collective-permute-start.19
  99.7 0.2 copy-done.11
  99.9 0.3 copy-done.7
  100.2 0.3 copy-done.8
  100.5 0.3 collective-permute-start.21
  100.8 1.0 copy.26
  101.8 0.7 broadcast_in_dim_tile.3.refs_3_
  102.5 0.6 stack.52.refs_0_
  103.1 1.0 collective-permute-done.21.refs_21_
  104.1 1.9 collective-permute-done.17.refs_17_
  106.0 2.4 %collective-permute-done.18.refs_18_ = bf16[608,1408]{1,0:T(8,128)(2,1)} collective-permute-done((bf16[608,1408]{1,0:T(8,128)(2,1)}, bf16[608,1408]{1,0:T(8,128)(2,1)}, u32[]{:S(2)}, u32[]{:S(2)}) %collective-permute-start.18) | collective-permute-done | bytes 1712160 | tf_op jit(solution)/shard_map/ppermute | solution.py:58
  108.4 2.4 %collective-permute-done.19.refs_19_ = bf16[608,1408]{1,0:T(8,128)(2,1)} collective-permute-done((bf16[608,1408]{1,0:T(8,128)(2,1)}, bf16[608,1408]{1,0:T(8,128)(2,1)}, u32[]{:S(2)}, u32[]{:S(2)}) %collective-permute-start.19) | collective-permute-done | bytes 1712160 | tf_op jit(solution)/shard_map/ppermute | solution.py:58
  110.9 26.8 %first_layer.3 = (bf16[256,2432]{1,0:T(8,128)(2,1)}, bf16[256,2432]{1,0:T(8,128)(2,1)}) custom-call(s32[10]{0:T(128)} %stack.52.refs_0_, bf16[2,256,2432]{2,1,0:T(8,128)(2,1)} %refs_1_.3, f32[2,3,2432]{2,1,0:T(4,128)} %bitcast.33, f32[1,1280]{1,0:T(1,128)} %broadcast_in_dim_tile.3.refs_3_, bf16[304,1408]{1,0:T(8,128)(2,1)} %copy-done.4, ...), custom_call_target="tpu_custom_call" | custom-call | tf_op jit(solution)/shard_map/first_layer/pallas_call | solution.py:360
  137.7 4.0 %collective-permute-start.23 = (bf16[256,2432]{1,0:T(8,128)(2,1)}, bf16[256,2432]{1,0:T(8,128)(2,1)S(1)}, u32[]{:S(2)}, u32[]{:S(2)}) collective-permute-start(bf16[256,2432]{1,0:T(8,128)(2,1)} %get-tuple-element.39), channel_id=1, source_target_pairs={{0,64},{1,65},{2,66},{3,67},{4,68},{5,69},{6,70},{7,71},{8,72},{9,... | collective-permute-start | bytes 3735560 | tf_op jit(solution)/shard_map/ppermute | solution.py:437
  141.7 26.7 %first_layer.2 = (bf16[256,2432]{1,0:T(8,128)(2,1)}, bf16[256,2432]{1,0:T(8,128)(2,1)}) custom-call(s32[10]{0:T(128)} %stack.52.refs_0_, bf16[2,256,2432]{2,1,0:T(8,128)(2,1)} %refs_1_.3, f32[2,3,2432]{2,1,0:T(4,128)} %bitcast.34, f32[1,1280]{1,0:T(1,128)} %broadcast_in_dim_tile.3.refs_3_, bf16[304,1408]{1,0:T(8,128)(2,1)} %copy-done.4, ...), custom_call_target="tpu_custom_call" | custom-call | tf_op jit(solution)/shard_map/first_layer/pallas_call | solution.py:360
  168.4 1.4 collective-permute-start.22
  169.8 1.1 copy.18.refs_27_
  170.9 1.0 copy-done.17
  172.0 29.5 %last_layer.2 = (bf16[128,64]{1,0:T(8,128)(2,1)}, bf16[2,256,2432]{2,1,0:T(8,128)(2,1)}, f32[128,64]{1,0:T(8,128)}) custom-call(s32[10]{0:T(128)} %stack.52.refs_0_, bf16[256,2432]{1,0:T(8,128)(2,1)} %copy-done.17, f32[2,3,2432]{2,1,0:T(4,128)} %bitcast.35, f32[1,1280]{1,0:T(1,128)} %broadcast_in_dim_tile.3.refs_3_, bf16[304,1408]{1,0:T(8,128)(2,1)} %copy-done.4, ...), custom_call_target="tpu_custom_call" | custom-call | tf_op jit(solution)/shard_map/last_layer/pallas_call | solution.py:360
  201.4 1.3 collective-permute-start.24
  202.8 0.1 copy.19
  202.9 1.1 copy-done.16
  204.0 29.2 %last_layer.3 = (bf16[128,64]{1,0:T(8,128)(2,1)}, bf16[2,256,2432]{2,1,0:T(8,128)(2,1)}, f32[128,64]{1,0:T(8,128)}) custom-call(s32[10]{0:T(128)} %stack.52.refs_0_, bf16[256,2432]{1,0:T(8,128)(2,1)} %copy-done.16, f32[2,3,2432]{2,1,0:T(4,128)} %bitcast.36, f32[1,1280]{1,0:T(1,128)} %broadcast_in_dim_tile.3.refs_3_, ...), custom_call_target="tpu_custom_call", output_to_operand_aliasing={{1}: (29, {})} | custom-call | tf_op jit(solution)/shard_map/last_layer/pallas_call | solution.py:360
  233.2 1.3 collective-permute-start.25
  234.6 4.7 %collective-permute-done.25 = bf16[128,64]{1,0:T(8,128)(2,1)S(1)} collective-permute-done((bf16[128,64]{1,0:T(8,128)(2,1)}, bf16[128,64]{1,0:T(8,128)(2,1)S(1)}, u32[]{:S(2)}, u32[]{:S(2)}) %collective-permute-start.25) | collective-permute-done | bytes 16416 | tf_op jit(solution)/shard_map/ppermute | solution.py:441
  239.3 0.1 multiply_subtract_fusion
  239.4 0.7 copy.21
  240.1 0.7 copy.22
  (65 shorter events, 0.4 us)
Async XLA Ops:
  0.6 6.4 %copy-start.14 = (bf16[1,1216,152]{1,2,0:T(8,128)(2,1)S(1)}, bf16[1,1216,152]{1,2,0:T(8,128)(2,1)}, u32[]{:S(2)}) copy-start(bf16[1,1216,152]{1,2,0:T(8,128)(2,1)} %param.17) | copy-start | bytes 1108996
  0.7 6.4 %copy-start.13 = (bf16[1,152,3648]{2,1,0:T(8,128)(2,1)S(1)}, bf16[1,152,3648]{2,1,0:T(8,128)(2,1)}, u32[]{:S(2)}) copy-start(bf16[1,152,3648]{2,1,0:T(8,128)(2,1)} %param.16) | copy-start | bytes 3326980
  3.6 3.4 %collective-permute-start = (bf16[152,2432]{1,0:T(8,128)(2,1)S(1)}, bf16[152,2432]{1,0:T(8,128)(2,1)S(1)}, u32[]{:S(2)}, u32[]{:S(2)}) collective-permute-start(bf16[152,2432]{1,0:T(8,128)(2,1)S(1)} %broadcast_select_fusion.4), channel_id=1, source_target_pairs={{0,1},{1,0},{2,3},{3,2},{4,5},{5,4},{6,7},{7,6},{8,9},{9,8},{10,11... | collective-permute-start | bytes 2217992 | tf_op jit(solution)/shard_map/ppermute | solution.py:58
  3.7 58.0 %collective-permute-start.14 = (bf16[2,256,2432]{2,1,0:T(8,128)(2,1)}, bf16[2,256,2432]{2,1,0:T(8,128)(2,1)S(1)}, u32[]{:S(2)}, u32[]{:S(2)}) collective-permute-start(bf16[2,256,2432]{2,1,0:T(8,128)(2,1)} %bitcast.39), channel_id=1, source_target_pairs={{0,16},{16,32},{32,48},{48,0},{1,17},{17,33},{33,49},{49,1},{2,18}... | collective-permute-start | bytes 7471112 | tf_op jit(solution)/shard_map/ppermute | solution.py:62
  5.5 56.3 %collective-permute-start.15 = (bf16[2,256,2432]{2,1,0:T(8,128)(2,1)}, bf16[2,256,2432]{2,1,0:T(8,128)(2,1)S(1)}, u32[]{:S(2)}, u32[]{:S(2)}) collective-permute-start(bf16[2,256,2432]{2,1,0:T(8,128)(2,1)} %bitcast.40), channel_id=1, source_target_pairs={{0,48},{16,0},{32,16},{48,32},{1,49},{17,1},{33,17},{49,33},{2,50}... | collective-permute-start | bytes 7471112 | tf_op jit(solution)/shard_map/ppermute | solution.py:62
  7.8 7.5 %copy-start.15 = (bf16[1,2,154,2432]{3,1,2,0:T(2,128)(2,1)S(1)}, bf16[1,2,154,2432]{3,1,2,0:T(2,128)(2,1)}, u32[]{:S(2)}) copy-start(bf16[1,2,154,2432]{3,1,2,0:T(2,128)(2,1)} %param.12) | copy-start | bytes 4494340
  7.9 17.2 %collective-permute-start.2 = (bf16[304,1024]{1,0:T(8,128)(2,1)S(1)}, bf16[304,1024]{1,0:T(8,128)(2,1)S(1)}, u32[]{:S(2)}, u32[]{:S(2)}) collective-permute-start(bf16[304,1024]{1,0:T(8,128)(2,1)S(1)} %pad_maximum_fusion.3), channel_id=1, source_target_pairs={{0,2},{1,3},{2,4},{3,5},{4,6},{5,7},{6,0},{7,1},{8,10},{9,11},{10,... | collective-permute-start | bytes 1867784 | tf_op jit(solution)/shard_map/ppermute | solution.py:50
  9.6 15.6 %collective-permute-start.3 = (bf16[304,1024]{1,0:T(8,128)(2,1)S(1)}, bf16[304,1024]{1,0:T(8,128)(2,1)S(1)}, u32[]{:S(2)}, u32[]{:S(2)}) collective-permute-start(bf16[304,1024]{1,0:T(8,128)(2,1)S(1)} %pad_maximum_fusion.3), channel_id=1, source_target_pairs={{0,6},{1,7},{2,0},{3,1},{4,2},{5,3},{6,4},{7,5},{8,14},{9,15},{10,... | collective-permute-start | bytes 1867784 | tf_op jit(solution)/shard_map/ppermute | solution.py:50
  11.3 71.7 %copy-start.4 = (bf16[304,1408]{1,0:T(8,128)(2,1)}, bf16[304,1408]{1,0:T(8,128)(2,1)S(1)}, u32[]{:S(2)}) copy-start(bf16[304,1408]{1,0:T(8,128)(2,1)S(1)} %fusion.refs_4_) | copy-start | bytes 2568196
  11.3 22.6 %collective-permute-start.1 = (bf16[304,1408]{1,0:T(8,128)(2,1)S(1)}, bf16[304,1408]{1,0:T(8,128)(2,1)S(1)}, u32[]{:S(2)}, u32[]{:S(2)}) collective-permute-start(bf16[304,1408]{1,0:T(8,128)(2,1)S(1)} %fusion.refs_4_), channel_id=1, source_target_pairs={{0,8},{1,9},{2,10},{3,11},{4,12},{5,13},{6,14},{7,15},{8,0},{9,1},... | collective-permute-start | bytes 2568200 | tf_op jit(solution)/shard_map/ppermute | solution.py:54
  25.2 12.3 %collective-permute-start.4 = (bf16[304,1024]{1,0:T(8,128)(2,1)S(1)}, bf16[304,1024]{1,0:T(8,128)(2,1)S(1)}, u32[]{:S(2)}, u32[]{:S(2)}) collective-permute-start(bf16[304,1024]{1,0:T(8,128)(2,1)S(1)} %broadcast_select_fusion.6), channel_id=1, source_target_pairs={{0,2},{1,7},{2,4},{3,1},{4,6},{5,3},{6,0},{7,5},{8,10},{9,15},{10,... | collective-permute-start | bytes 1867784 | tf_op jit(solution)/shard_map/ppermute | solution.py:72
  33.9 49.1 %copy-start.6 = (bf16[304,1408]{1,0:T(8,128)(2,1)}, bf16[304,1408]{1,0:T(8,128)(2,1)S(1)}, u32[]{:S(2)}) copy-start(bf16[304,1408]{1,0:T(8,128)(2,1)S(1)} %collective-permute-done.1.refs_5_) | copy-start | bytes 2568196
  34.0 39.5 %collective-permute-start.5 = (bf16[608,1408]{1,0:T(8,128)(2,1)S(1)}, bf16[608,1408]{1,0:T(8,128)(2,1)}, u32[]{:S(2)}, u32[]{:S(2)}) collective-permute-start(bf16[608,1408]{1,0:T(8,128)(2,1)S(1)} %pad_maximum_fusion.1), channel_id=1, source_target_pairs={{0,2},{1,3},{2,4},{3,5},{4,6},{5,7},{6,0},{7,1},{8,10},{9,11},{10,... | collective-permute-start | bytes 5136392 | tf_op jit(solution)/shard_map/ppermute | solution.py:50
  34.4 39.1 %collective-permute-start.6 = (bf16[608,1408]{1,0:T(8,128)(2,1)S(1)}, bf16[608,1408]{1,0:T(8,128)(2,1)}, u32[]{:S(2)}, u32[]{:S(2)}) collective-permute-start(bf16[608,1408]{1,0:T(8,128)(2,1)S(1)} %pad_maximum_fusion.1), channel_id=1, source_target_pairs={{0,6},{1,7},{2,0},{3,1},{4,2},{5,3},{6,4},{7,5},{8,14},{9,15},{10,... | collective-permute-start | bytes 5136392 | tf_op jit(solution)/shard_map/ppermute | solution.py:50
  37.5 56.8 %copy-start.2 = (bf16[912,1024]{1,0:T(8,128)(2,1)}, bf16[912,1024]{1,0:T(8,128)(2,1)S(1)}, u32[]{:S(2)}) copy-start(bf16[912,1024]{1,0:T(8,128)(2,1)S(1)} %pad_maximum_fusion.refs_6_) | copy-start | bytes 5603332
  37.5 57.9 %copy-start.9 = (bf16[304,1024]{1,0:T(8,128)(2,1)}, bf16[304,1024]{1,0:T(8,128)(2,1)S(1)}, u32[]{:S(2)}) copy-start(bf16[304,1024]{1,0:T(8,128)(2,1)S(1)} %collective-permute-done.4.refs_7_) | copy-start | bytes 1867780
  37.5 42.5 %collective-permute-start.8 = (bf16[912,1024]{1,0:T(8,128)(2,1)S(1)}, bf16[912,1024]{1,0:T(8,128)(2,1)}, u32[]{:S(2)}, u32[]{:S(2)}) collective-permute-start(bf16[912,1024]{1,0:T(8,128)(2,1)S(1)} %pad_maximum_fusion.refs_6_), channel_id=1, source_target_pairs={{0,8},{1,9},{2,10},{3,11},{4,12},{5,13},{6,14},{7,15},{8,0},{9,1},... | collective-permute-start | bytes 5603336 | tf_op jit(solution)/shard_map/ppermute | solution.py:54
  61.8 1.5 copy-start
  61.8 2.2 copy-start.1
  64.0 36.8 %copy-start.21 = (f32[1,2,3,2432]{3,1,2,0:T(2,128)S(1)}, f32[1,2,3,2432]{3,1,2,0:T(2,128)}, u32[]{:S(2)}) copy-start(f32[1,2,3,2432]{3,1,2,0:T(2,128)} %param.14) | copy-start | bytes 175108
  64.0 37.8 %copy-start.22 = (f32[1,64]{1,0:T(1,128)S(1)}, f32[1,64]{1,0:T(1,128)}, u32[]{:S(2)}) copy-start(f32[1,64]{1,0:T(1,128)} %param.15) | copy-start | bytes 772
  64.0 31.5 %collective-permute-start.16 = (bf16[2,256,2432]{2,1,0:T(8,128)(2,1)S(1)}, bf16[2,256,2432]{2,1,0:T(8,128)(2,1)S(1)}, u32[]{:S(2)}, u32[]{:S(2)}) collective-permute-start(bf16[2,256,2432]{2,1,0:T(8,128)(2,1)S(1)} %broadcast_select_fusion), channel_id=1, source_target_pairs={{0,16},{1,49},{2,18},{3,51},{4,20},{5,53},{6,22},{7,55},{8,24},{9,... | collective-permute-start | bytes 7471112 | tf_op jit(solution)/shard_map/ppermute | solution.py:81
  75.2 23.3 %collective-permute-start.7 = (bf16[608,1408]{1,0:T(8,128)(2,1)S(1)}, bf16[608,1408]{1,0:T(8,128)(2,1)}, u32[]{:S(2)}, u32[]{:S(2)}) collective-permute-start(bf16[608,1408]{1,0:T(8,128)(2,1)S(1)} %broadcast_select_fusion.1), channel_id=1, source_target_pairs={{0,2},{1,7},{2,4},{3,1},{4,6},{5,3},{6,0},{7,5},{8,10},{9,15},{10,... | collective-permute-start | bytes 5136392 | tf_op jit(solution)/shard_map/ppermute | solution.py:72
  80.0 14.3 %collective-permute-start.9 = (bf16[304,1024]{1,0:T(8,128)(2,1)S(1)}, bf16[304,1024]{1,0:T(8,128)(2,1)S(1)}, u32[]{:S(2)}, u32[]{:S(2)}) collective-permute-start(bf16[304,1024]{1,0:T(8,128)(2,1)S(1)} %collective-permute-done.4.refs_7_), channel_id=1, source_target_pairs={{0,8},{1,9},{2,10},{3,11},{4,12},{5,13},{6,14},{7,15},{8,0},{9,1},... | collective-permute-start | bytes 1867784 | tf_op jit(solution)/shard_map/ppermute | solution.py:54
  83.0 16.2 %collective-permute-start.11 = (bf16[304,1408]{1,0:T(8,128)(2,1)S(1)}, bf16[304,1408]{1,0:T(8,128)(2,1)S(1)}, u32[]{:S(2)}, u32[]{:S(2)}) collective-permute-start(bf16[304,1408]{1,0:T(8,128)(2,1)S(1)} %collective-permute-done.1.refs_5_), channel_id=1, source_target_pairs={{0,1},{1,0},{2,3},{3,2},{4,5},{5,4},{6,7},{7,6},{8,9},{9,8},{10,11... | collective-permute-start | bytes 2568200 | tf_op jit(solution)/shard_map/ppermute | solution.py:58
  83.0 16.6 %collective-permute-start.10 = (bf16[304,1408]{1,0:T(8,128)(2,1)S(1)}, bf16[304,1408]{1,0:T(8,128)(2,1)S(1)}, u32[]{:S(2)}, u32[]{:S(2)}) collective-permute-start(bf16[304,1408]{1,0:T(8,128)(2,1)S(1)} %fusion.refs_4_), channel_id=1, source_target_pairs={{0,1},{1,0},{2,3},{3,2},{4,5},{5,4},{6,7},{7,6},{8,9},{9,8},{10,11... | collective-permute-start | bytes 2568200 | tf_op jit(solution)/shard_map/ppermute | solution.py:58
  94.3 16.6 %copy-start.10 = (bf16[304,1024]{1,0:T(8,128)(2,1)}, bf16[304,1024]{1,0:T(8,128)(2,1)S(1)}, u32[]{:S(2)}) copy-start(bf16[304,1024]{1,0:T(8,128)(2,1)S(1)} %collective-permute-done.9.refs_12_) | copy-start | bytes 1867780
  94.3 5.4 %collective-permute-start.12 = (bf16[912,1024]{1,0:T(8,128)(2,1)S(1)}, bf16[912,1024]{1,0:T(8,128)(2,1)S(1)}, u32[]{:S(2)}, u32[]{:S(2)}) collective-permute-start(bf16[912,1024]{1,0:T(8,128)(2,1)S(1)} %pad_maximum_fusion.refs_6_), channel_id=1, source_target_pairs={{0,1},{1,0},{2,3},{3,2},{4,5},{5,4},{6,7},{7,6},{8,9},{9,8},{10,11... | collective-permute-start | bytes 5603336 | tf_op jit(solution)/shard_map/ppermute | solution.py:58
  95.5 4.3 %copy-start.3 = (bf16[2,256,2432]{2,1,0:T(8,128)(2,1)}, bf16[2,256,2432]{2,1,0:T(8,128)(2,1)S(1)}, u32[]{:S(2)}) copy-start(bf16[2,256,2432]{2,1,0:T(8,128)(2,1)S(1)} %collective-permute-done.16.refs_24_) | copy-start | bytes 7471108
  95.5 3.6 %collective-permute-start.13 = (bf16[304,1024]{1,0:T(8,128)(2,1)S(1)}, bf16[304,1024]{1,0:T(8,128)(2,1)S(1)}, u32[]{:S(2)}, u32[]{:S(2)}) collective-permute-start(bf16[304,1024]{1,0:T(8,128)(2,1)S(1)} %collective-permute-done.4.refs_7_), channel_id=1, source_target_pairs={{0,1},{1,0},{2,3},{3,2},{4,5},{5,4},{6,7},{7,6},{8,9},{9,8},{10,11... | collective-permute-start | bytes 1867784 | tf_op jit(solution)/shard_map/ppermute | solution.py:58
  98.5 12.4 %collective-permute-start.20 = (bf16[912,1024]{1,0:T(8,128)(2,1)}, bf16[912,1024]{1,0:T(8,128)(2,1)}, u32[]{:S(2)}, u32[]{:S(2)}) collective-permute-start(bf16[912,1024]{1,0:T(8,128)(2,1)} %collective-permute-done.8.refs_11_), channel_id=1, source_target_pairs={{0,1},{1,0},{2,3},{3,2},{4,5},{5,4},{6,7},{7,6},{8,9},{9,8},{10,11... | collective-permute-start | bytes 5603336 | tf_op jit(solution)/shard_map/ppermute | solution.py:58
  99.1 0.8 copy-start.11
  99.1 6.9 %collective-permute-start.17 = (bf16[608,1408]{1,0:T(8,128)(2,1)}, bf16[608,1408]{1,0:T(8,128)(2,1)}, u32[]{:S(2)}, u32[]{:S(2)}) collective-permute-start(bf16[608,1408]{1,0:T(8,128)(2,1)} %collective-permute-done.5.refs_8_), channel_id=1, source_target_pairs={{0,1},{1,0},{2,3},{3,2},{4,5},{5,4},{6,7},{7,6},{8,9},{9,8},{10,11... | collective-permute-start | bytes 5136392 | tf_op jit(solution)/shard_map/ppermute | solution.py:58
  99.2 1.0 copy-start.7
  99.2 9.2 %collective-permute-start.18 = (bf16[608,1408]{1,0:T(8,128)(2,1)}, bf16[608,1408]{1,0:T(8,128)(2,1)}, u32[]{:S(2)}, u32[]{:S(2)}) collective-permute-start(bf16[608,1408]{1,0:T(8,128)(2,1)} %collective-permute-done.6.refs_9_), channel_id=1, source_target_pairs={{0,1},{1,0},{2,3},{3,2},{4,5},{5,4},{6,7},{7,6},{8,9},{9,8},{10,11... | collective-permute-start | bytes 5136392 | tf_op jit(solution)/shard_map/ppermute | solution.py:58
  99.6 0.9 copy-start.8
  99.6 11.3 %collective-permute-start.19 = (bf16[608,1408]{1,0:T(8,128)(2,1)}, bf16[608,1408]{1,0:T(8,128)(2,1)}, u32[]{:S(2)}, u32[]{:S(2)}) collective-permute-start(bf16[608,1408]{1,0:T(8,128)(2,1)} %collective-permute-done.7.refs_10_), channel_id=1, source_target_pairs={{0,1},{1,0},{2,3},{3,2},{4,5},{5,4},{6,7},{7,6},{8,9},{9,8},{10,11... | collective-permute-start | bytes 5136392 | tf_op jit(solution)/shard_map/ppermute | solution.py:58
  100.5 10.4 %copy-start.5 = (bf16[912,1024]{1,0:T(8,128)(2,1)}, bf16[912,1024]{1,0:T(8,128)(2,1)S(1)}, u32[]{:S(2)}) copy-start(bf16[912,1024]{1,0:T(8,128)(2,1)S(1)} %collective-permute-done.12.refs_15_) | copy-start | bytes 5603332
  100.5 3.6 %collective-permute-start.21 = (bf16[304,1024]{1,0:T(8,128)(2,1)S(1)}, bf16[304,1024]{1,0:T(8,128)(2,1)S(1)}, u32[]{:S(2)}, u32[]{:S(2)}) collective-permute-start(bf16[304,1024]{1,0:T(8,128)(2,1)S(1)} %collective-permute-done.9.refs_12_), channel_id=1, source_target_pairs={{0,1},{1,0},{2,3},{3,2},{4,5},{5,4},{6,7},{7,6},{8,9},{9,8},{10,11... | collective-permute-start | bytes 1867784 | tf_op jit(solution)/shard_map/ppermute | solution.py:58
  104.1 6.8 %copy-start.12 = (bf16[304,1024]{1,0:T(8,128)(2,1)}, bf16[304,1024]{1,0:T(8,128)(2,1)S(1)}, u32[]{:S(2)}) copy-start(bf16[304,1024]{1,0:T(8,128)(2,1)S(1)} %collective-permute-done.21.refs_21_) | copy-start | bytes 1867780
  137.7 32.1 %copy-start.18 = (bf16[2432,64]{0,1:T(8,128)(2,1)S(1)}, bf16[2432,64]{0,1:T(8,128)(2,1)}, u32[]{:S(2)}) copy-start(bf16[2432,64]{0,1:T(8,128)(2,1)} %param.19) | copy-start | bytes 933892
  137.7 33.2 %collective-permute-start.23 = (bf16[256,2432]{1,0:T(8,128)(2,1)}, bf16[256,2432]{1,0:T(8,128)(2,1)S(1)}, u32[]{:S(2)}, u32[]{:S(2)}) collective-permute-start(bf16[256,2432]{1,0:T(8,128)(2,1)} %get-tuple-element.39), channel_id=1, source_target_pairs={{0,64},{1,65},{2,66},{3,67},{4,68},{5,69},{6,70},{7,71},{8,72},{9,... | collective-permute-start | bytes 3735560 | tf_op jit(solution)/shard_map/ppermute | solution.py:437
  168.4 34.4 %collective-permute-start.22 = (bf16[256,2432]{1,0:T(8,128)(2,1)}, bf16[256,2432]{1,0:T(8,128)(2,1)S(1)}, u32[]{:S(2)}, u32[]{:S(2)}) collective-permute-start(bf16[256,2432]{1,0:T(8,128)(2,1)} %get-tuple-element.37), channel_id=1, source_target_pairs={{0,64},{1,65},{2,66},{3,67},{4,68},{5,69},{6,70},{7,71},{8,72},{9,... | collective-permute-start | bytes 3735560 | tf_op jit(solution)/shard_map/ppermute | solution.py:437
  170.9 1.0 copy-start.17
  171.9 30.8 %copy-start.23 = (s32[2]{0:T(128)S(1)}, s32[2]{0:T(128)}, u32[]{:S(2)}) copy-start(s32[2]{0:T(128)} %param.21) | copy-start | bytes 28
  172.0 30.8 %copy-start.19 = (f32[2,128,64]{1,2,0:T(8,128)S(1)}, f32[2,128,64]{1,2,0:T(8,128)}, u32[]{:S(2)}) copy-start(f32[2,128,64]{1,2,0:T(8,128)} %param.20) | copy-start | bytes 196612
  201.4 33.1 %collective-permute-start.24 = (bf16[128,64]{1,0:T(8,128)(2,1)}, bf16[128,64]{1,0:T(8,128)(2,1)S(1)}, u32[]{:S(2)}, u32[]{:S(2)}) collective-permute-start(bf16[128,64]{1,0:T(8,128)(2,1)} %get-tuple-element.43), channel_id=1, source_target_pairs={{64,0},{65,1},{66,2},{67,3},{68,4},{69,5},{70,6},{71,7},{72,8},{73... | collective-permute-start | bytes 49160 | tf_op jit(solution)/shard_map/ppermute | solution.py:441
  202.9 1.1 copy-start.16
  204.0 30.6 %copy-start.20 = (f32[128,64]{1,0:T(8,128)S(1)}, f32[128,64]{1,0:T(8,128)}, u32[]{:S(2)}) copy-start(f32[128,64]{1,0:T(8,128)} %get-tuple-element.44) | copy-start | bytes 98308
  233.2 6.0 %collective-permute-start.25 = (bf16[128,64]{1,0:T(8,128)(2,1)}, bf16[128,64]{1,0:T(8,128)(2,1)S(1)}, u32[]{:S(2)}, u32[]{:S(2)}) collective-permute-start(bf16[128,64]{1,0:T(8,128)(2,1)} %get-tuple-element.45), channel_id=1, source_target_pairs={{64,0},{65,1},{66,2},{67,3},{68,4},{69,5},{70,6},{71,7},{72,8},{73... | collective-permute-start | bytes 49160 | tf_op jit(solution)/shard_map/ppermute | solution.py:441

commit v2 on v1

--- a/solution.py
+++ b/solution.py
@@ -31,52 +31,33 @@
     return flow_shift * s / (1.0 + (flow_shift - 1.0) * s)
 
 
-def shard_pairs(flip_z=0, dx=0, flip_core=0):
+def shard_pairs(flip_z=0, flip_core=0):
+    return [(i, i ^ (8 * flip_z) ^ flip_core) for i in range(16)]
+
+
+def z_flip(value):
+    return lax.ppermute(value, "shard", shard_pairs(flip_z=1))
+
+
+def core_flip(value):
+    return lax.ppermute(value, "shard", shard_pairs(flip_core=1))
+
+
+def x_turn(value, step):
     pairs = []
     for z in range(2):
         for x in range(4):
             for c in range(2):
-                src = z * 8 + x * 2 + c
-                dst = (z ^ flip_z) * 8 + ((x + dx) % 4) * 2 + (c ^ flip_core)
-                pairs.append((src, dst))
-    return pairs
-
-
-def ring_pairs(step):
-    return [(i, (i + step) % 4) for i in range(4)]
-
-
-def x_shift(value, dx):
-    return lax.ppermute(value, "shard", shard_pairs(dx=dx))
-
-
-def z_flip(value):
-    return lax.ppermute(value, "shard", shard_pairs(flip_z=1))
-
-
-def core_flip(value):
-    return lax.ppermute(value, "shard", shard_pairs(flip_core=1))
-
-
-def y_shift(value, dy):
-    return lax.ppermute(value, "patch", ring_pairs(dy))
-
-
-def x_relay(value):
-    pairs = []
-    for z in range(2):
-        for x in range(4):
-            for c in range(2):
-                dx = 1 if c == 0 else -1
+                dx = step if c == 0 else -step
                 pairs.append((z * 8 + x * 2 + c, z * 8 + ((x + dx) % 4) * 2 + c))
     return lax.ppermute(value, "shard", pairs)
 
 
-def y_relay(value):
+def y_turn(value, step):
     pairs = []
     for y in range(4):
         for k in range(16):
-            dy = 1 if k % 2 == 0 else -1
+            dy = step if k % 2 == 0 else -step
             pairs.append((y * 16 + k, ((y + dy) % 4) * 16 + k))
     return lax.ppermute(value, ("patch", "shard"), pairs)
 
@@ -110,11 +91,11 @@
 
 def layer_kernel(final, req, *refs):
     sc, x_hbm, mod_ref, gain_ref = refs[:4]
-    mine = refs[4:13]
-    theirs = refs[13:22]
-    stale = refs[22:25]
-    text_ref = refs[25]
-    refs = refs[26:]
+    mine = refs[4:11]
+    theirs = refs[11:18]
+    stale = refs[18:21]
+    text_ref = refs[21]
+    refs = refs[22:]
     mod_ref = mod_ref.at[req]
     if final:
         fmod_ref, fw_ref, early_ref = refs[0].at[req], refs[1], refs[2]
@@ -135,19 +116,20 @@
             sem,
         ).start()
 
-    def spread_z(pieces, col, count, dst, dst_col, sem):
-        put(pieces[0], 0, col, count, dst, 0, 0, dst_col, sem)
-        put(pieces[1], 0, col, count, dst, 1, 0, dst_col, sem)
-        for j, ref in enumerate(pieces[4:7]):
+    kv_order, oq_order = (0, 1, 2, 3), (0, 2, 1, 3)
+
+    def spread_z(pieces, order, col, count, dst, dst_col, sem):
+        for j, ref in zip(order, pieces[:4]):
             for slot in range(2):
-                put(ref, slot * BLK, col, count, dst, slot, j + 1, dst_col, sem)
-
-    def spread_x(pieces, dst, dst_col, sem):
-        for slot in range(2):
-            three, far = pieces[(2, 7)[slot]], pieces[(3, 8)[slot]]
-            for j in range(3):
-                put(three, j * BLK, 0, XC, dst, slot, j, dst_col, sem)
-            put(far, 0, 0, XC, dst, slot, 3, dst_col, sem)
+                put(ref, slot * BLK, col, count, dst, slot, j, dst_col, sem)
+
+    def spread_x(pieces, order, dst, dst_col, sem):
+        four, three, far = pieces[4:]
+        for i in range(4):
+            put(four, i * BLK, 0, XC, dst, 0, order[i], dst_col, sem)
+        for i in range(3):
+            put(three, i * BLK, 0, XC, dst, 1, order[i], dst_col, sem)
+        put(far, 0, 0, XC, dst, 1, 3, dst_col, sem)
 
     def by_core(step):
         @pl.when(sc[0] == 0)
@@ -159,17 +141,17 @@
             step(theirs, mine)
 
     def fetch_kv_z(kv_pieces, oq_pieces):
-        spread_z(kv_pieces, 0, ZC, w_kv, 0, sems.at[0])
+        spread_z(kv_pieces, kv_order, 0, ZC, w_kv, 0, sems.at[0])
 
     def fetch_kv_x(kv_pieces, oq_pieces):
-        spread_x(kv_pieces, w_kv, ZC, sems.at[1])
+        spread_x(kv_pieces, kv_order, w_kv, ZC, sems.at[1])
 
     def fetch_q(kv_pieces, oq_pieces):
-        spread_z(oq_pieces, 0, WIDE, w_q, 0, sems.at[2])
+        spread_z(oq_pieces, oq_order, 0, WIDE, w_q, 0, sems.at[2])
 
     def fetch_out(kv_pieces, oq_pieces):
-        spread_z(oq_pieces, D - WIDE, ZC + WIDE - D, w_o, 0, sems.at[4])
-        spread_x(oq_pieces, w_o, ZC + WIDE - D, sems.at[4])
+        spread_z(oq_pieces, oq_order, D - WIDE, ZC + WIDE - D, w_o, 0, sems.at[4])
+        spread_x(oq_pieces, oq_order, w_o, ZC + WIDE - D, sems.at[4])
 
     def fetch_keys():
         for j, ref in enumerate((*stale, text_ref)):
@@ -325,7 +307,7 @@
     hbm = pl.BlockSpec(memory_space=pl.ANY)
     final = last is not None
     operands = [scalars, x, mod, gain, *mine, *theirs, *stale, text]
-    specs = [pl.BlockSpec(memory_space=pltpu.SMEM), hbm, vmem, vmem] + [hbm] * 22
+    specs = [pl.BlockSpec(memory_space=pltpu.SMEM), hbm, vmem, vmem] + [hbm] * 18
     scratch = [
         pltpu.VMEM((D, D), jnp.bfloat16),
         pltpu.VMEM((D, WIDE), jnp.bfloat16),
@@ -397,28 +379,31 @@
     near_z, near_x = mine_block[:, :ZC], mine_block[:, ZC:]
     text = jnp.pad(text_kv[0], ((0, 0), (0, TXT_PAD - TXT), (0, 0)))
 
-    before_x, after_x = x_shift(near_x, 1), x_shift(near_x, -1)
+    one_x = x_turn(near_x, 1)
     opposite_z = z_flip(near_z)
-    before_y, after_y = y_shift(stale_kv[0], 1), y_shift(stale_kv[0], -1)
-    far_x = x_relay(jnp.where(core == 0, after(before_x, text), after_x))
-    three_x = jnp.concatenate([near_x, before_x, after_x], 0)
+    one_y = y_turn(stale_kv[0], 1)
+    two_x = x_turn(near_x, -1)
+    far_x = x_turn(after(one_x, text), 1)
+    two_y = y_turn(after(stale_kv[0], one_y), -1)
+    far_y = y_turn(one_y, 1)
+    three_x = jnp.concatenate([near_x, one_x, two_x], 0)
     opposite_three = z_flip(three_x)
     pair_z = jnp.concatenate([near_z, opposite_z], 0)
-    before_z, after_z = x_shift(pair_z, 1), x_shift(pair_z, -1)
-    far_y = y_relay(jnp.where(core == 0, after(before_y, far_x), after_y))
-    far_z = x_relay(jnp.where(core == 0, before_z, after_z))
+    one_z, two_z = x_turn(pair_z, 1), x_turn(pair_z, -1)
+    far_z = x_turn(one_z, 1)
     opposite_far = z_flip(after(far_x, opposite_three))
-    early = (near_z, opposite_z, three_x, far_x)
-    their_early = tuple(core_flip(after(piece, before_z)) for piece in early)
-    their_before_z = core_flip(after(before_z, far_y))
-    their_after_z = core_flip(after(after_z, far_y))
+    four_x = jnp.concatenate([three_x, far_x], 0)
+    their_pair = core_flip(after(pair_z, far_x))
+    their_four_x = core_flip(after(four_x, far_x))
+    their_one_z = core_flip(after(one_z, two_y))
+    their_two_z = core_flip(after(two_z, two_y))
     their_far_z = core_flip(after(far_z, far_y))
     their_opposite_three = core_flip(after(opposite_three, far_y))
     their_opposite_far = core_flip(after(opposite_far, far_y))
-    mine = (*early, before_z, after_z, far_z, opposite_three, opposite_far)
-    theirs = (*their_early, their_before_z, their_after_z, their_far_z,
-              their_opposite_three, their_opposite_far)
-    stale = (before_y, after_y, far_y)
+    mine = (pair_z, one_z, two_z, far_z, four_x, opposite_three, opposite_far)
+    theirs = (their_pair, their_one_z, their_two_z, their_far_z,
+              their_four_x, their_opposite_three, their_opposite_far)
+    stale = (one_y, two_y, far_y)
     gain = jnp.tile(score_gain[0] * (1.0 / math.sqrt(HEAD)), WIDE // HEAD)[None, :]
     rows = [
         ((z_hi ^ slot) * 4 + (x_at + dx) % 4) * BLK for slot in range(2) for dx in (0, 3, 1, 2)

time: 241 us -> 252 us (1.046)
  waiting for transfers between devices: 77 us -> 90 us
    ppermute x9, waiting for transfers between devices: 41.4 us -> 76 us  [the longest x6 54.3 us: x_turn(): return lax.ppermute(value, 'shard', pairs)]
    ppermute x3, waiting for transfers between devices: 22.5 us -> 1.9 us  [z_flip(): return lax.ppermute(value, 'shard', shard_pairs(flip_z=1))]
    ppermute x3, starting transfers between devices: 11 us -> 8.18 us  [z_flip(): return lax.ppermute(value, 'shard', shard_pairs(flip_z=1))]
    ppermute x10 -> x8, waiting for transfers between devices: 8.38 us -> 7.39 us  [core_flip(): return lax.ppermute(value, 'shard', shard_pairs(flip_core=1))]
    unnamed x54 -> x46, local copies, waits for them, and re-layouts: 8.68 us -> 8.11 us
  transfers between devices with their start and end apart: 26 -> 24, of which waited for: 14 -> 10; matrix products, arithmetic and copies ran while one was open for 3% -> 2% of each run, Pallas kernels for 35% -> 34%
where the time goes in v2:
time: 252 us; the launch traced here: 251 us
  Pallas kernels  112 us (44%)
  waiting for transfers between devices  90 us (36%)
  starting transfers between devices  32.8 us (13%)
  local copies, waits for them, and re-layouts  11.8 us (5%)
  other arithmetic  3.45 us (1%)
    pallas_call x4, Pallas kernels, run_layer(): pl.pallas_call(lambda *refs: layer_kernel(final, req, *refs), name='last_...  112 us
    ppermute x6, waiting for transfers between devices, x_turn(): return lax.ppermute(value, 'shard', pairs)  54.3 us
    ppermute x3, waiting for transfers between devices, y_turn(): return lax.ppermute(value, ('patch', 'shard'), pairs)  21.7 us
    ppermute x6, starting transfers between devices, x_turn(): return lax.ppermute(value, 'shard', pairs)  8.45 us
    ppermute x3, starting transfers between devices, z_flip(): return lax.ppermute(value, 'shard', shard_pairs(flip_z=1))  8.18 us
    unnamed x46, local copies, waits for them, and re-layouts  8.11 us
    ppermute x8, waiting for transfers between devices, core_flip(): return lax.ppermute(value, 'shard', shard_pairs(flip_core=1))  7.39 us
    ppermute x3, starting transfers between devices, y_turn(): return lax.ppermute(value, ('patch', 'shard'), pairs)  5.9 us
  transfers between devices with their start and end apart: 24, of which 10 were waited for; matrix products, arithmetic and copies ran while one was open for 2% of the time, Pallas kernels for 34%

profile of v2, /device:TPU:0, one launch (start us, length us, event | category | flops | bytes accessed | tf_op | source)
XLA Modules:
  0.0 251.2 jit_solution(8229134030517467038)
XLA Ops:
  0.6 0.0 copy-start.8
  0.6 0.0 copy-start.9
  0.7 1.1 slice.17
  1.8 1.8 broadcast_select_fusion.2
  3.6 0.1 collective-permute-start
  3.7 1.7 collective-permute-start.11
  5.5 0.5 collective-permute-done
  5.9 0.8 broadcast_select_fusion
  6.7 0.1 fusion
  6.8 4.0 %collective-permute-start.1 = (bf16[304,1408]{1,0:T(8,128)(2,1)S(1)}, bf16[304,1408]{1,0:T(8,128)(2,1)S(1)}, u32[]{:S(2)}, u32[]{:S(2)}) collective-permute-start(bf16[304,1408]{1,0:T(8,128)(2,1)S(1)} %fusion), channel_id=1, source_target_pairs={{0,8},{1,9},{2,10},{3,11},{4,12},{5,13},{6,14},{7,15},{8,0},{9,1},... | collective-permute-start | bytes 2568200 | tf_op jit(solution)/shard_map/ppermute | solution.py:39
  10.8 0.1 pad_maximum_fusion.4
  10.9 1.6 collective-permute-start.5
  12.4 1.7 collective-permute-start.6
  14.2 12.5 %collective-permute-done.5 = bf16[304,1024]{1,0:T(8,128)(2,1)S(1)} collective-permute-done((bf16[304,1024]{1,0:T(8,128)(2,1)S(1)}, bf16[304,1024]{1,0:T(8,128)(2,1)S(1)}, u32[]{:S(2)}, u32[]{:S(2)}) %collective-permute-start.5) | collective-permute-done | bytes 622624 | tf_op jit(solution)/shard_map/ppermute | solution.py:53
  26.7 1.2 collective-permute-done.6
  27.9 0.1 pad_maximum_fusion.1
  28.1 0.0 copy-start.10
  28.1 0.4 collective-permute-start.8
  28.5 1.9 collective-permute-done.1
  30.4 0.1 pad_maximum_fusion.2.refs_4_
  30.5 1.6 collective-permute-start.2
  32.1 0.2 copy.25
  32.2 0.0 copy-start.17
  32.2 1.3 pad.4.refs_21_
  33.5 1.5 collective-permute-start.7
  35.0 1.7 collective-permute-start.3
  36.7 1.4 collective-permute-start.15
  38.1 40.6 %collective-permute-done.7 = bf16[304,1024]{1,0:T(8,128)(2,1)S(1)} collective-permute-done((bf16[304,1024]{1,0:T(8,128)(2,1)S(1)}, bf16[304,1024]{1,0:T(8,128)(2,1)S(1)}, u32[]{:S(2)}, u32[]{:S(2)}) %collective-permute-start.7) | collective-permute-done | bytes 622624 | tf_op jit(solution)/shard_map/ppermute | solution.py:53
  78.7 2.8 %collective-permute-start.12 = (bf16[2,256,2432]{2,1,0:T(8,128)(2,1)S(1)}, bf16[2,256,2432]{2,1,0:T(8,128)(2,1)S(1)}, u32[]{:S(2)}, u32[]{:S(2)}) collective-permute-start(bf16[2,256,2432]{2,1,0:T(8,128)(2,1)S(1)} %bitcast.40), channel_id=1, source_target_pairs={{0,48},{1,17},{2,50},{3,19},{4,52},{5,21},{6,54},{7,23},{8,56},{9,... | collective-permute-start | bytes 7471112 | tf_op jit(solution)/shard_map/ppermute | solution.py:62
  81.5 0.0 collective-permute-done.8.refs_9_
  81.5 0.3 collective-permute-start.4
  81.9 0.3 pad_maximum_fusion.refs_8_
  82.2 1.5 collective-permute-start.17
  83.8 3.8 %collective-permute-start.9 = (bf16[304,1024]{1,0:T(8,128)(2,1)S(1)}, bf16[304,1024]{1,0:T(8,128)(2,1)S(1)}, u32[]{:S(2)}, u32[]{:S(2)}) collective-permute-start(bf16[304,1024]{1,0:T(8,128)(2,1)S(1)} %collective-permute-done.7), channel_id=1, source_target_pairs={{0,8},{1,9},{2,10},{3,11},{4,12},{5,13},{6,14},{7,15},{8,0},{9,1},... | collective-permute-start | bytes 1867784 | tf_op jit(solution)/shard_map/ppermute | solution.py:39
  87.6 21.7 %collective-permute-done.12.refs_19_ = bf16[2,256,2432]{2,1,0:T(8,128)(2,1)S(1)} collective-permute-done((bf16[2,256,2432]{2,1,0:T(8,128)(2,1)S(1)}, bf16[2,256,2432]{2,1,0:T(8,128)(2,1)S(1)}, u32[]{:S(2)}, u32[]{:S(2)}) %collective-permute-start.12) | collective-permute-done | bytes 2490400 | tf_op jit(solution)/shard_map/ppermute | solution.py:62
  109.3 0.5 collective-permute-start.13
  109.8 0.1 collective-permute-start.14
  109.9 0.4 collective-permute-start.16
  110.3 0.5 copy-done.4
  110.8 0.5 copy-done.6
  111.3 1.5 copy-done.5
  112.8 0.7 copy.26
  113.5 0.7 broadcast_in_dim_tile.3.refs_3_
  114.2 0.6 stack.52.refs_0_
  114.8 2.7 %collective-permute-done.19.refs_17_ = bf16[304,1024]{1,0:T(8,128)(2,1)} collective-permute-done((bf16[304,1024]{1,0:T(8,128)(2,1)S(1)}, bf16[304,1024]{1,0:T(8,128)(2,1)}, u32[]{:S(2)}, u32[]{:S(2)}) %collective-permute-start.19) | collective-permute-done | bytes 622624 | tf_op jit(solution)/shard_map/ppermute | solution.py:43
  117.5 1.8 collective-permute-done.14.refs_13_
  119.2 2.4 collective-permute-done.16.refs_14_
  121.7 26.8 %first_layer.3 = (bf16[256,2432]{1,0:T(8,128)(2,1)}, bf16[256,2432]{1,0:T(8,128)(2,1)}) custom-call(s32[10]{0:T(128)} %stack.52.refs_0_, bf16[2,256,2432]{2,1,0:T(8,128)(2,1)} %refs_1_.3, f32[2,3,2432]{2,1,0:T(4,128)} %bitcast.33, f32[1,1280]{1,0:T(1,128)} %broadcast_in_dim_tile.3.refs_3_, bf16[608,1408]{1,0:T(8,128)(2,1)} %copy-done.1, ...), custom_call_target="tpu_custom_call" | custom-call | tf_op jit(solution)/shard_map/first_layer/pallas_call | solution.py:342
  148.5 0.0 copy-start.13
  148.5 3.6 %collective-permute-start.21 = (bf16[256,2432]{1,0:T(8,128)(2,1)}, bf16[256,2432]{1,0:T(8,128)(2,1)S(1)}, u32[]{:S(2)}, u32[]{:S(2)}) collective-permute-start(bf16[256,2432]{1,0:T(8,128)(2,1)} %get-tuple-element.35), channel_id=1, source_target_pairs={{0,64},{1,65},{2,66},{3,67},{4,68},{5,69},{6,70},{7,71},{8,72},{9,... | collective-permute-start | bytes 3735560 | tf_op jit(solution)/shard_map/ppermute | solution.py:422
  152.1 26.6 %first_layer.2 = (bf16[256,2432]{1,0:T(8,128)(2,1)}, bf16[256,2432]{1,0:T(8,128)(2,1)}) custom-call(s32[10]{0:T(128)} %stack.52.refs_0_, bf16[2,256,2432]{2,1,0:T(8,128)(2,1)} %refs_1_.3, f32[2,3,2432]{2,1,0:T(4,128)} %bitcast.34, f32[1,1280]{1,0:T(1,128)} %broadcast_in_dim_tile.3.refs_3_, bf16[608,1408]{1,0:T(8,128)(2,1)} %copy-done.1, ...), custom_call_target="tpu_custom_call" | custom-call | tf_op jit(solution)/shard_map/first_layer/pallas_call | solution.py:342
  178.8 1.4 collective-permute-start.20
  180.2 1.1 copy.18.refs_23_
  181.3 1.0 copy-done.12
  182.4 29.5 %last_layer.2 = (bf16[128,64]{1,0:T(8,128)(2,1)}, bf16[2,256,2432]{2,1,0:T(8,128)(2,1)}, f32[128,64]{1,0:T(8,128)}) custom-call(s32[10]{0:T(128)} %stack.52.refs_0_, bf16[256,2432]{1,0:T(8,128)(2,1)} %copy-done.12, f32[2,3,2432]{2,1,0:T(4,128)} %bitcast.35, f32[1,1280]{1,0:T(1,128)} %broadcast_in_dim_tile.3.refs_3_, bf16[608,1408]{1,0:T(8,128)(2,1)} %copy-done.1, ...), custom_call_target="tpu_custom_call" | custom-call | tf_op jit(solution)/shard_map/last_layer/pallas_call | solution.py:342
  211.8 1.3 collective-permute-start.22
  213.2 0.1 copy.19
  213.3 1.1 copy-done.11
  214.4 29.3 %last_layer.3 = (bf16[128,64]{1,0:T(8,128)(2,1)}, bf16[2,256,2432]{2,1,0:T(8,128)(2,1)}, f32[128,64]{1,0:T(8,128)}) custom-call(s32[10]{0:T(128)} %stack.52.refs_0_, bf16[256,2432]{1,0:T(8,128)(2,1)} %copy-done.11, f32[2,3,2432]{2,1,0:T(4,128)} %bitcast.36, f32[1,1280]{1,0:T(1,128)} %broadcast_in_dim_tile.3.refs_3_, ...), custom_call_target="tpu_custom_call", output_to_operand_aliasing={{1}: (25, {})} | custom-call | tf_op jit(solution)/shard_map/last_layer/pallas_call | solution.py:342
  243.6 1.3 collective-permute-start.23
  245.0 4.7 %collective-permute-done.23 = bf16[128,64]{1,0:T(8,128)(2,1)S(1)} collective-permute-done((bf16[128,64]{1,0:T(8,128)(2,1)}, bf16[128,64]{1,0:T(8,128)(2,1)S(1)}, u32[]{:S(2)}, u32[]{:S(2)}) %collective-permute-start.23) | collective-permute-done | bytes 16416 | tf_op jit(solution)/shard_map/ppermute | solution.py:426
  249.7 0.1 multiply_subtract_fusion
  249.8 0.7 copy.21
  250.5 0.7 copy.22
  (51 shorter events, 0.1 us)
Async XLA Ops:
  0.6 5.3 %copy-start.8 = (bf16[1,152,3648]{2,1,0:T(8,128)(2,1)S(1)}, bf16[1,152,3648]{2,1,0:T(8,128)(2,1)}, u32[]{:S(2)}) copy-start(bf16[1,152,3648]{2,1,0:T(8,128)(2,1)} %param.16) | copy-start | bytes 3326980
  0.6 5.3 %copy-start.9 = (bf16[1,1216,152]{1,2,0:T(8,128)(2,1)S(1)}, bf16[1,1216,152]{1,2,0:T(8,128)(2,1)}, u32[]{:S(2)}) copy-start(bf16[1,1216,152]{1,2,0:T(8,128)(2,1)} %param.17) | copy-start | bytes 1108996
  3.6 2.3 collective-permute-start
  3.7 33.0 %collective-permute-start.11 = (bf16[2,256,2432]{2,1,0:T(8,128)(2,1)}, bf16[2,256,2432]{2,1,0:T(8,128)(2,1)S(1)}, u32[]{:S(2)}, u32[]{:S(2)}) collective-permute-start(bf16[2,256,2432]{2,1,0:T(8,128)(2,1)} %bitcast.39), channel_id=1, source_target_pairs={{0,16},{1,49},{2,18},{3,51},{4,20},{5,53},{6,22},{7,55},{8,24},{9,... | collective-permute-start | bytes 7471112 | tf_op jit(solution)/shard_map/ppermute | solution.py:62
  6.8 23.6 %collective-permute-start.1 = (bf16[304,1408]{1,0:T(8,128)(2,1)S(1)}, bf16[304,1408]{1,0:T(8,128)(2,1)S(1)}, u32[]{:S(2)}, u32[]{:S(2)}) collective-permute-start(bf16[304,1408]{1,0:T(8,128)(2,1)S(1)} %fusion), channel_id=1, source_target_pairs={{0,8},{1,9},{2,10},{3,11},{4,12},{5,13},{6,14},{7,15},{8,0},{9,1},... | collective-permute-start | bytes 2568200 | tf_op jit(solution)/shard_map/ppermute | solution.py:39
  10.9 15.9 %collective-permute-start.5 = (bf16[304,1024]{1,0:T(8,128)(2,1)S(1)}, bf16[304,1024]{1,0:T(8,128)(2,1)S(1)}, u32[]{:S(2)}, u32[]{:S(2)}) collective-permute-start(bf16[304,1024]{1,0:T(8,128)(2,1)S(1)} %pad_maximum_fusion.4), channel_id=1, source_target_pairs={{0,2},{1,7},{2,4},{3,1},{4,6},{5,3},{6,0},{7,5},{8,10},{9,15},{10,... | collective-permute-start | bytes 1867784 | tf_op jit(solution)/shard_map/ppermute | solution.py:53
  12.4 15.5 %collective-permute-start.6 = (bf16[304,1024]{1,0:T(8,128)(2,1)S(1)}, bf16[304,1024]{1,0:T(8,128)(2,1)S(1)}, u32[]{:S(2)}, u32[]{:S(2)}) collective-permute-start(bf16[304,1024]{1,0:T(8,128)(2,1)S(1)} %pad_maximum_fusion.4), channel_id=1, source_target_pairs={{0,6},{1,3},{2,0},{3,5},{4,2},{5,7},{6,4},{7,1},{8,14},{9,11},{10,... | collective-permute-start | bytes 1867784 | tf_op jit(solution)/shard_map/ppermute | solution.py:53
  28.1 4.0 %copy-start.10 = (bf16[1,2,154,2432]{3,1,2,0:T(2,128)(2,1)S(1)}, bf16[1,2,154,2432]{3,1,2,0:T(2,128)(2,1)}, u32[]{:S(2)}) copy-start(bf16[1,2,154,2432]{3,1,2,0:T(2,128)(2,1)} %param.12) | copy-start | bytes 4494340
  28.1 53.4 %collective-permute-start.8 = (bf16[912,1024]{1,0:T(8,128)(2,1)S(1)}, bf16[912,1024]{1,0:T(8,128)(2,1)}, u32[]{:S(2)}, u32[]{:S(2)}) collective-permute-start(bf16[912,1024]{1,0:T(8,128)(2,1)S(1)} %pad_maximum_fusion.1), channel_id=1, source_target_pairs={{0,8},{1,9},{2,10},{3,11},{4,12},{5,13},{6,14},{7,15},{8,0},{9,1},... | collective-permute-start | bytes 5603336 | tf_op jit(solution)/shard_map/ppermute | solution.py:39
  30.5 51.0 %copy-start.1 = (bf16[608,1408]{1,0:T(8,128)(2,1)}, bf16[608,1408]{1,0:T(8,128)(2,1)S(1)}, u32[]{:S(2)}) copy-start(bf16[608,1408]{1,0:T(8,128)(2,1)S(1)} %pad_maximum_fusion.2.refs_4_) | copy-start | bytes 5136388
  30.5 51.0 %collective-permute-start.2 = (bf16[608,1408]{1,0:T(8,128)(2,1)S(1)}, bf16[608,1408]{1,0:T(8,128)(2,1)}, u32[]{:S(2)}, u32[]{:S(2)}) collective-permute-start(bf16[608,1408]{1,0:T(8,128)(2,1)S(1)} %pad_maximum_fusion.2.refs_4_), channel_id=1, source_target_pairs={{0,2},{1,7},{2,4},{3,1},{4,6},{5,3},{6,0},{7,5},{8,10},{9,15},{10,... | collective-permute-start | bytes 5136392 | tf_op jit(solution)/shard_map/ppermute | solution.py:53
  32.2 46.5 %copy-start.17 = (bf16[1,2,256,2432]{3,2,1,0:T(8,128)(2,1)S(1)}, bf16[1,2,256,2432]{3,2,1,0:T(8,128)(2,1)}, u32[]{:S(2)}) copy-start(bf16[1,2,256,2432]{3,2,1,0:T(8,128)(2,1)} %param.13) | copy-start | bytes 7471108
  33.5 79.3 %copy-start.16 = (f32[1,2,3,2432]{3,1,2,0:T(2,128)S(1)}, f32[1,2,3,2432]{3,1,2,0:T(2,128)}, u32[]{:S(2)}) copy-start(f32[1,2,3,2432]{3,1,2,0:T(2,128)} %param.14) | copy-start | bytes 175108
  33.5 80.0 %copy-start.18 = (f32[1,64]{1,0:T(1,128)S(1)}, f32[1,64]{1,0:T(1,128)}, u32[]{:S(2)}) copy-start(f32[1,64]{1,0:T(1,128)} %param.15) | copy-start | bytes 772
  33.5 45.2 %collective-permute-start.7 = (bf16[304,1024]{1,0:T(8,128)(2,1)S(1)}, bf16[304,1024]{1,0:T(8,128)(2,1)S(1)}, u32[]{:S(2)}, u32[]{:S(2)}) collective-permute-start(bf16[304,1024]{1,0:T(8,128)(2,1)S(1)} %collective-permute-done.5), channel_id=1, source_target_pairs={{0,2},{1,7},{2,4},{3,1},{4,6},{5,3},{6,0},{7,5},{8,10},{9,15},{10,... | collective-permute-start | bytes 1867784 | tf_op jit(solution)/shard_map/ppermute | solution.py:53
  35.0 47.3 %collective-permute-start.3 = (bf16[608,1408]{1,0:T(8,128)(2,1)S(1)}, bf16[608,1408]{1,0:T(8,128)(2,1)}, u32[]{:S(2)}, u32[]{:S(2)}) collective-permute-start(bf16[608,1408]{1,0:T(8,128)(2,1)S(1)} %pad_maximum_fusion.2.refs_4_), channel_id=1, source_target_pairs={{0,6},{1,3},{2,0},{3,5},{4,2},{5,7},{6,4},{7,1},{8,14},{9,11},{10,... | collective-permute-start | bytes 5136392 | tf_op jit(solution)/shard_map/ppermute | solution.py:53
  36.7 45.5 %copy-start.2 = (bf16[2,256,2432]{2,1,0:T(8,128)(2,1)}, bf16[2,256,2432]{2,1,0:T(8,128)(2,1)S(1)}, u32[]{:S(2)}) copy-start(bf16[2,256,2432]{2,1,0:T(8,128)(2,1)S(1)} %collective-permute-done.11.refs_18_) | copy-start | bytes 7471108
  36.7 47.1 %collective-permute-start.15 = (bf16[2,256,2432]{2,1,0:T(8,128)(2,1)S(1)}, bf16[2,256,2432]{2,1,0:T(8,128)(2,1)S(1)}, u32[]{:S(2)}, u32[]{:S(2)}) collective-permute-start(bf16[2,256,2432]{2,1,0:T(8,128)(2,1)S(1)} %collective-permute-done.11.refs_18_), channel_id=1, source_target_pairs={{0,16},{1,49},{2,18},{3,51},{4,20},{5,53},{6,22},{7,55},{8,24},{9,... | collective-permute-start | bytes 7471112 | tf_op jit(solution)/shard_map/ppermute | solution.py:62
  78.7 30.6 %collective-permute-start.12 = (bf16[2,256,2432]{2,1,0:T(8,128)(2,1)S(1)}, bf16[2,256,2432]{2,1,0:T(8,128)(2,1)S(1)}, u32[]{:S(2)}, u32[]{:S(2)}) collective-permute-start(bf16[2,256,2432]{2,1,0:T(8,128)(2,1)S(1)} %bitcast.40), channel_id=1, source_target_pairs={{0,48},{1,17},{2,50},{3,19},{4,52},{5,21},{6,54},{7,23},{8,56},{9,... | collective-permute-start | bytes 7471112 | tf_op jit(solution)/shard_map/ppermute | solution.py:62
  81.5 28.3 %collective-permute-start.10 = (bf16[608,1408]{1,0:T(8,128)(2,1)S(1)}, bf16[608,1408]{1,0:T(8,128)(2,1)S(1)}, u32[]{:S(2)}, u32[]{:S(2)}) collective-permute-start(bf16[608,1408]{1,0:T(8,128)(2,1)S(1)} %pad_maximum_fusion.2.refs_4_), channel_id=1, source_target_pairs={{0,1},{1,0},{2,3},{3,2},{4,5},{5,4},{6,7},{7,6},{8,9},{9,8},{10,11... | collective-permute-start | bytes 5136392 | tf_op jit(solution)/shard_map/ppermute | solution.py:43
  81.5 27.8 %collective-permute-start.4 = (bf16[608,1408]{1,0:T(8,128)(2,1)}, bf16[608,1408]{1,0:T(8,128)(2,1)}, u32[]{:S(2)}, u32[]{:S(2)}) collective-permute-start(bf16[608,1408]{1,0:T(8,128)(2,1)} %collective-permute-done.2.refs_5_), channel_id=1, source_target_pairs={{0,2},{1,7},{2,4},{3,1},{4,6},{5,3},{6,0},{7,5},{8,10},{9,15},{10,... | collective-permute-start | bytes 5136392 | tf_op jit(solution)/shard_map/ppermute | solution.py:53
  82.2 39.5 %copy-start = (bf16[1216,1024]{1,0:T(8,128)(2,1)}, bf16[1216,1024]{1,0:T(8,128)(2,1)S(1)}, u32[]{:S(2)}) copy-start(bf16[1216,1024]{1,0:T(8,128)(2,1)S(1)} %pad_maximum_fusion.refs_8_) | copy-start | bytes 7471108
  82.2 28.1 %collective-permute-start.17 = (bf16[1216,1024]{1,0:T(8,128)(2,1)S(1)}, bf16[1216,1024]{1,0:T(8,128)(2,1)S(1)}, u32[]{:S(2)}, u32[]{:S(2)}) collective-permute-start(bf16[1216,1024]{1,0:T(8,128)(2,1)S(1)} %pad_maximum_fusion.refs_8_), channel_id=1, source_target_pairs={{0,1},{1,0},{2,3},{3,2},{4,5},{5,4},{6,7},{7,6},{8,9},{9,8},{10,11... | collective-permute-start | bytes 7471112 | tf_op jit(solution)/shard_map/ppermute | solution.py:43
  83.8 26.5 %copy-start.3 = (bf16[2,256,2432]{2,1,0:T(8,128)(2,1)}, bf16[2,256,2432]{2,1,0:T(8,128)(2,1)S(1)}, u32[]{:S(2)}) copy-start(bf16[2,256,2432]{2,1,0:T(8,128)(2,1)S(1)} %collective-permute-done.15.refs_20_) | copy-start | bytes 7471108
  83.8 26.1 %collective-permute-start.9 = (bf16[304,1024]{1,0:T(8,128)(2,1)S(1)}, bf16[304,1024]{1,0:T(8,128)(2,1)S(1)}, u32[]{:S(2)}, u32[]{:S(2)}) collective-permute-start(bf16[304,1024]{1,0:T(8,128)(2,1)S(1)} %collective-permute-done.7), channel_id=1, source_target_pairs={{0,8},{1,9},{2,10},{3,11},{4,12},{5,13},{6,14},{7,15},{8,0},{9,1},... | collective-permute-start | bytes 1867784 | tf_op jit(solution)/shard_map/ppermute | solution.py:39
  109.3 1.5 copy-start.4
  109.3 12.4 %collective-permute-start.18 = (bf16[912,1024]{1,0:T(8,128)(2,1)}, bf16[912,1024]{1,0:T(8,128)(2,1)}, u32[]{:S(2)}, u32[]{:S(2)}) collective-permute-start(bf16[912,1024]{1,0:T(8,128)(2,1)} %collective-permute-done.8.refs_9_), channel_id=1, source_target_pairs={{0,1},{1,0},{2,3},{3,2},{4,5},{5,4},{6,7},{7,6},{8,9},{9,8},{10,11... | collective-permute-start | bytes 5603336 | tf_op jit(solution)/shard_map/ppermute | solution.py:43
  109.3 8.2 %collective-permute-start.13 = (bf16[608,1408]{1,0:T(8,128)(2,1)}, bf16[608,1408]{1,0:T(8,128)(2,1)}, u32[]{:S(2)}, u32[]{:S(2)}) collective-permute-start(bf16[608,1408]{1,0:T(8,128)(2,1)} %collective-permute-done.2.refs_5_), channel_id=1, source_target_pairs={{0,1},{1,0},{2,3},{3,2},{4,5},{5,4},{6,7},{7,6},{8,9},{9,8},{10,11... | collective-permute-start | bytes 5136392 | tf_op jit(solution)/shard_map/ppermute | solution.py:43
  109.8 1.5 copy-start.6
  109.8 9.4 %collective-permute-start.14 = (bf16[608,1408]{1,0:T(8,128)(2,1)}, bf16[608,1408]{1,0:T(8,128)(2,1)}, u32[]{:S(2)}, u32[]{:S(2)}) collective-permute-start(bf16[608,1408]{1,0:T(8,128)(2,1)} %collective-permute-done.3.refs_6_), channel_id=1, source_target_pairs={{0,1},{1,0},{2,3},{3,2},{4,5},{5,4},{6,7},{7,6},{8,9},{9,8},{10,11... | collective-permute-start | bytes 5136392 | tf_op jit(solution)/shard_map/ppermute | solution.py:43
  109.9 11.8 %copy-start.7 = (bf16[304,1024]{1,0:T(8,128)(2,1)}, bf16[304,1024]{1,0:T(8,128)(2,1)S(1)}, u32[]{:S(2)}) copy-start(bf16[304,1024]{1,0:T(8,128)(2,1)S(1)} %collective-permute-done.9.refs_10_) | copy-start | bytes 1867780
  109.9 11.8 %collective-permute-start.16 = (bf16[608,1408]{1,0:T(8,128)(2,1)}, bf16[608,1408]{1,0:T(8,128)(2,1)}, u32[]{:S(2)}, u32[]{:S(2)}) collective-permute-start(bf16[608,1408]{1,0:T(8,128)(2,1)} %collective-permute-done.4.refs_7_), channel_id=1, source_target_pairs={{0,1},{1,0},{2,3},{3,2},{4,5},{5,4},{6,7},{7,6},{8,9},{9,8},{10,11... | collective-permute-start | bytes 5136392 | tf_op jit(solution)/shard_map/ppermute | solution.py:43
  111.3 1.5 copy-start.5
  112.8 4.7 %collective-permute-start.19 = (bf16[304,1024]{1,0:T(8,128)(2,1)S(1)}, bf16[304,1024]{1,0:T(8,128)(2,1)}, u32[]{:S(2)}, u32[]{:S(2)}) collective-permute-start(bf16[304,1024]{1,0:T(8,128)(2,1)S(1)} %collective-permute-done.9.refs_10_), channel_id=1, source_target_pairs={{0,1},{1,0},{2,3},{3,2},{4,5},{5,4},{6,7},{7,6},{8,9},{9,8},{10,11... | collective-permute-start | bytes 1867784 | tf_op jit(solution)/shard_map/ppermute | solution.py:43
  148.5 31.7 %copy-start.13 = (bf16[2432,64]{0,1:T(8,128)(2,1)S(1)}, bf16[2432,64]{0,1:T(8,128)(2,1)}, u32[]{:S(2)}) copy-start(bf16[2432,64]{0,1:T(8,128)(2,1)} %param.19) | copy-start | bytes 933892
  148.5 32.8 %collective-permute-start.21 = (bf16[256,2432]{1,0:T(8,128)(2,1)}, bf16[256,2432]{1,0:T(8,128)(2,1)S(1)}, u32[]{:S(2)}, u32[]{:S(2)}) collective-permute-start(bf16[256,2432]{1,0:T(8,128)(2,1)} %get-tuple-element.35), channel_id=1, source_target_pairs={{0,64},{1,65},{2,66},{3,67},{4,68},{5,69},{6,70},{7,71},{8,72},{9,... | collective-permute-start | bytes 3735560 | tf_op jit(solution)/shard_map/ppermute | solution.py:422
  178.8 34.5 %collective-permute-start.20 = (bf16[256,2432]{1,0:T(8,128)(2,1)}, bf16[256,2432]{1,0:T(8,128)(2,1)S(1)}, u32[]{:S(2)}, u32[]{:S(2)}) collective-permute-start(bf16[256,2432]{1,0:T(8,128)(2,1)} %get-tuple-element.33), channel_id=1, source_target_pairs={{0,64},{1,65},{2,66},{3,67},{4,68},{5,69},{6,70},{7,71},{8,72},{9,... | collective-permute-start | bytes 3735560 | tf_op jit(solution)/shard_map/ppermute | solution.py:422
  181.3 1.0 copy-start.12
  182.4 30.8 %copy-start.19 = (s32[2]{0:T(128)S(1)}, s32[2]{0:T(128)}, u32[]{:S(2)}) copy-start(s32[2]{0:T(128)} %param.21) | copy-start | bytes 28
  182.4 30.8 %copy-start.14 = (f32[2,128,64]{1,2,0:T(8,128)S(1)}, f32[2,128,64]{1,2,0:T(8,128)}, u32[]{:S(2)}) copy-start(f32[2,128,64]{1,2,0:T(8,128)} %param.20) | copy-start | bytes 196612
  211.8 33.1 %collective-permute-start.22 = (bf16[128,64]{1,0:T(8,128)(2,1)}, bf16[128,64]{1,0:T(8,128)(2,1)S(1)}, u32[]{:S(2)}, u32[]{:S(2)}) collective-permute-start(bf16[128,64]{1,0:T(8,128)(2,1)} %get-tuple-element.39), channel_id=1, source_target_pairs={{64,0},{65,1},{66,2},{67,3},{68,4},{69,5},{70,6},{71,7},{72,8},{73... | collective-permute-start | bytes 49160 | tf_op jit(solution)/shard_map/ppermute | solution.py:426
  213.3 1.1 copy-start.11
  214.4 30.6 %copy-start.15 = (f32[128,64]{1,0:T(8,128)S(1)}, f32[128,64]{1,0:T(8,128)}, u32[]{:S(2)}) copy-start(f32[128,64]{1,0:T(8,128)} %get-tuple-element.40) | copy-start | bytes 98308
  243.6 6.0 %collective-permute-start.23 = (bf16[128,64]{1,0:T(8,128)(2,1)}, bf16[128,64]{1,0:T(8,128)(2,1)S(1)}, u32[]{:S(2)}, u32[]{:S(2)}) collective-permute-start(bf16[128,64]{1,0:T(8,128)(2,1)} %get-tuple-element.41), channel_id=1, source_target_pairs={{64,0},{65,1},{66,2},{67,3},{68,4},{69,5},{70,6},{71,7},{72,8},{73... | collective-permute-start | bytes 49160 | tf_op jit(solution)/shard_map/ppermute | solution.py:426

commit v3 on v1

--- a/solution.py
+++ b/solution.py
@@ -110,11 +110,11 @@
 
 def layer_kernel(final, req, *refs):
     sc, x_hbm, mod_ref, gain_ref = refs[:4]
-    mine = refs[4:13]
-    theirs = refs[13:22]
-    stale = refs[22:25]
-    text_ref = refs[25]
-    refs = refs[26:]
+    mine = refs[4:11]
+    theirs = refs[11:18]
+    stale = refs[18:21]
+    text_ref = refs[21]
+    refs = refs[22:]
     mod_ref = mod_ref.at[req]
     if final:
         fmod_ref, fw_ref, early_ref = refs[0].at[req], refs[1], refs[2]
@@ -136,18 +136,17 @@
         ).start()
 
     def spread_z(pieces, col, count, dst, dst_col, sem):
-        put(pieces[0], 0, col, count, dst, 0, 0, dst_col, sem)
-        put(pieces[1], 0, col, count, dst, 1, 0, dst_col, sem)
-        for j, ref in enumerate(pieces[4:7]):
+        for j, ref in enumerate(pieces[:4]):
             for slot in range(2):
-                put(ref, slot * BLK, col, count, dst, slot, j + 1, dst_col, sem)
+                put(ref, slot * BLK, col, count, dst, slot, j, dst_col, sem)
 
     def spread_x(pieces, dst, dst_col, sem):
-        for slot in range(2):
-            three, far = pieces[(2, 7)[slot]], pieces[(3, 8)[slot]]
-            for j in range(3):
-                put(three, j * BLK, 0, XC, dst, slot, j, dst_col, sem)
-            put(far, 0, 0, XC, dst, slot, 3, dst_col, sem)
+        four, three, far = pieces[4:]
+        for j in range(4):
+            put(four, j * BLK, 0, XC, dst, 0, j, dst_col, sem)
+        for j in range(3):
+            put(three, j * BLK, 0, XC, dst, 1, j, dst_col, sem)
+        put(far, 0, 0, XC, dst, 1, 3, dst_col, sem)
 
     def by_core(step):
         @pl.when(sc[0] == 0)
@@ -325,7 +324,7 @@
     hbm = pl.BlockSpec(memory_space=pl.ANY)
     final = last is not None
     operands = [scalars, x, mod, gain, *mine, *theirs, *stale, text]
-    specs = [pl.BlockSpec(memory_space=pltpu.SMEM), hbm, vmem, vmem] + [hbm] * 22
+    specs = [pl.BlockSpec(memory_space=pltpu.SMEM), hbm, vmem, vmem] + [hbm] * 18
     scratch = [
         pltpu.VMEM((D, D), jnp.bfloat16),
         pltpu.VMEM((D, WIDE), jnp.bfloat16),
@@ -408,16 +407,17 @@
     far_y = y_relay(jnp.where(core == 0, after(before_y, far_x), after_y))
     far_z = x_relay(jnp.where(core == 0, before_z, after_z))
     opposite_far = z_flip(after(far_x, opposite_three))
-    early = (near_z, opposite_z, three_x, far_x)
-    their_early = tuple(core_flip(after(piece, before_z)) for piece in early)
+    four_x = jnp.concatenate([three_x, far_x], 0)
+    their_pair = core_flip(after(pair_z, before_z))
+    their_four_x = core_flip(after(four_x, before_z))
     their_before_z = core_flip(after(before_z, far_y))
     their_after_z = core_flip(after(after_z, far_y))
     their_far_z = core_flip(after(far_z, far_y))
     their_opposite_three = core_flip(after(opposite_three, far_y))
     their_opposite_far = core_flip(after(opposite_far, far_y))
-    mine = (*early, before_z, after_z, far_z, opposite_three, opposite_far)
-    theirs = (*their_early, their_before_z, their_after_z, their_far_z,
-              their_opposite_three, their_opposite_far)
+    mine = (pair_z, before_z, after_z, far_z, four_x, opposite_three, opposite_far)
+    theirs = (their_pair, their_before_z, their_after_z, their_far_z,
+              their_four_x, their_opposite_three, their_opposite_far)
     stale = (before_y, after_y, far_y)
     gain = jnp.tile(score_gain[0] * (1.0 / math.sqrt(HEAD)), WIDE // HEAD)[None, :]
     rows = [

time: 241 us -> 238 us (0.988)
  waiting for transfers between devices: 77 us -> 72.9 us
    ppermute x10 -> x8, waiting for transfers between devices: 8.38 us -> 4.75 us  [core_flip(): return lax.ppermute(value, 'shard', shard_pairs(flip_core=1))]
    unnamed x54 -> x44, local copies, waits for them, and re-layouts: 8.68 us -> 9.1 us
  transfers between devices with their start and end apart: 26 -> 24, of which waited for: 14 -> 11; matrix products, arithmetic and copies ran while one was open for 3% -> 3% of each run, Pallas kernels for 35% -> 36%
where the time goes in v3:
time: 238 us
  Pallas kernels  112 us (47%)
  waiting for transfers between devices  72.9 us (31%)
  starting transfers between devices  33.5 us (14%)
  local copies, waits for them, and re-layouts  12.9 us (5%)
  other arithmetic  5.39 us (2%)
    pallas_call x4, Pallas kernels, run_layer(): pl.pallas_call(lambda *refs: layer_kernel(final, req, *refs), name='last_...  112 us
    ppermute x3, waiting for transfers between devices, z_flip(): return lax.ppermute(value, 'shard', shard_pairs(flip_z=1))  22.5 us
    ppermute x2, waiting for transfers between devices, y_shift(): return lax.ppermute(value, 'patch', ring_pairs(dy))  20.2 us
    ppermute x4, waiting for transfers between devices, x_shift(): return lax.ppermute(value, 'shard', shard_pairs(dx=dx))  17 us
    ppermute x3, starting transfers between devices, z_flip(): return lax.ppermute(value, 'shard', shard_pairs(flip_z=1))  11 us
    unnamed x44, local copies, waits for them, and re-layouts  9.1 us
    ppermute x4, starting transfers between devices, x_shift(): return lax.ppermute(value, 'shard', shard_pairs(dx=dx))  6.61 us
    ppermute x2, starting transfers between devices, on_device(): arrived.append(lax.ppermute(x_next, 'section', [(0, 1)]))  5.42 us
  transfers between devices with their start and end apart: 24, of which 11 were waited for; matrix products, arithmetic and copies ran while one was open for 3% of the time, Pallas kernels for 36%

profile of v3, /device:TPU:0, one launch (start us, length us, event | category | flops | bytes accessed | tf_op | source)
XLA Modules:
  0.0 237.8 jit_solution(5918318661440402260)
XLA Ops:
  0.7 1.1 slice.17
  1.8 1.8 broadcast_select_fusion.4
  3.6 0.1 collective-permute-start
  3.7 1.7 collective-permute-start.11
  5.5 1.6 collective-permute-start.12
  7.0 0.8 broadcast_select_fusion.2
  7.8 0.1 pad_maximum_fusion.4
  7.9 1.6 collective-permute-start.5
  9.6 1.7 collective-permute-start.6
  11.2 0.1 fusion
  11.3 4.0 %collective-permute-start.1 = (bf16[304,1408]{1,0:T(8,128)(2,1)S(1)}, bf16[304,1408]{1,0:T(8,128)(2,1)S(1)}, u32[]{:S(2)}, u32[]{:S(2)}) collective-permute-start(bf16[304,1408]{1,0:T(8,128)(2,1)S(1)} %fusion), channel_id=1, source_target_pairs={{0,8},{1,9},{2,10},{3,11},{4,12},{5,13},{6,14},{7,15},{8,0},{9,1},... | collective-permute-start | bytes 2568200 | tf_op jit(solution)/shard_map/ppermute | solution.py:54
  15.3 0.2 copy.25
  15.5 1.3 pad.4.refs_21_
  16.7 8.4 %collective-permute-done.5 = bf16[304,1024]{1,0:T(8,128)(2,1)S(1)} collective-permute-done((bf16[304,1024]{1,0:T(8,128)(2,1)S(1)}, bf16[304,1024]{1,0:T(8,128)(2,1)S(1)}, u32[]{:S(2)}, u32[]{:S(2)}) %collective-permute-start.5) | collective-permute-done | bytes 622624 | tf_op jit(solution)/shard_map/ppermute | solution.py:50
  25.1 0.1 broadcast_select_fusion.6
  25.2 1.6 collective-permute-start.7
  26.8 7.1 %collective-permute-done.1 = bf16[304,1408]{1,0:T(8,128)(2,1)S(1)} collective-permute-done((bf16[304,1408]{1,0:T(8,128)(2,1)S(1)}, bf16[304,1408]{1,0:T(8,128)(2,1)S(1)}, u32[]{:S(2)}, u32[]{:S(2)}) %collective-permute-start.1) | collective-permute-done | bytes 856096 | tf_op jit(solution)/shard_map/ppermute | solution.py:54
  33.9 0.1 pad_maximum_fusion.2.refs_4_
  34.0 0.3 collective-permute-start.2
  34.4 3.0 %collective-permute-start.3 = (bf16[608,1408]{1,0:T(8,128)(2,1)S(1)}, bf16[608,1408]{1,0:T(8,128)(2,1)}, u32[]{:S(2)}, u32[]{:S(2)}) collective-permute-start(bf16[608,1408]{1,0:T(8,128)(2,1)S(1)} %pad_maximum_fusion.2.refs_4_), channel_id=1, source_target_pairs={{0,6},{1,7},{2,0},{3,1},{4,2},{5,3},{6,4},{7,5},{8,14},{9,15},{10,... | collective-permute-start | bytes 5136392 | tf_op jit(solution)/shard_map/ppermute | solution.py:50
  37.3 0.1 pad_maximum_fusion.1
  37.5 4.0 %collective-permute-start.8 = (bf16[912,1024]{1,0:T(8,128)(2,1)S(1)}, bf16[912,1024]{1,0:T(8,128)(2,1)}, u32[]{:S(2)}, u32[]{:S(2)}) collective-permute-start(bf16[912,1024]{1,0:T(8,128)(2,1)S(1)} %pad_maximum_fusion.1), channel_id=1, source_target_pairs={{0,8},{1,9},{2,10},{3,11},{4,12},{5,13},{6,14},{7,15},{8,0},{9,1},... | collective-permute-start | bytes 5603336 | tf_op jit(solution)/shard_map/ppermute | solution.py:54
  41.5 20.2 %collective-permute-done.11.refs_18_ = bf16[2,256,2432]{2,1,0:T(8,128)(2,1)S(1)} collective-permute-done((bf16[2,256,2432]{2,1,0:T(8,128)(2,1)}, bf16[2,256,2432]{2,1,0:T(8,128)(2,1)S(1)}, u32[]{:S(2)}, u32[]{:S(2)}) %collective-permute-start.11) | collective-permute-done | bytes 2490400 | tf_op jit(solution)/shard_map/ppermute | solution.py:62
  61.8 0.0 collective-permute-done.12.refs_19_
  61.8 0.3 broadcast_select_fusion
  62.1 1.2 copy-done.1
  63.2 0.8 copy-done.2
  64.0 0.9 collective-permute-start.13
  64.9 8.6 %collective-permute-done.2.refs_5_ = bf16[608,1408]{1,0:T(8,128)(2,1)} collective-permute-done((bf16[608,1408]{1,0:T(8,128)(2,1)S(1)}, bf16[608,1408]{1,0:T(8,128)(2,1)}, u32[]{:S(2)}, u32[]{:S(2)}) %collective-permute-start.2) | collective-permute-done | bytes 1712160 | tf_op jit(solution)/shard_map/ppermute | solution.py:50
  73.5 1.6 broadcast_select_fusion.1
  75.2 0.3 collective-permute-start.4
  75.5 4.5 %collective-permute-done.8.refs_9_ = bf16[912,1024]{1,0:T(8,128)(2,1)} collective-permute-done((bf16[912,1024]{1,0:T(8,128)(2,1)S(1)}, bf16[912,1024]{1,0:T(8,128)(2,1)}, u32[]{:S(2)}, u32[]{:S(2)}) %collective-permute-start.8) | collective-permute-done | bytes 1867808 | tf_op jit(solution)/shard_map/ppermute | solution.py:54
  80.0 2.9 %collective-permute-start.9 = (bf16[304,1024]{1,0:T(8,128)(2,1)S(1)}, bf16[304,1024]{1,0:T(8,128)(2,1)S(1)}, u32[]{:S(2)}, u32[]{:S(2)}) collective-permute-start(bf16[304,1024]{1,0:T(8,128)(2,1)S(1)} %collective-permute-done.7), channel_id=1, source_target_pairs={{0,8},{1,9},{2,10},{3,11},{4,12},{5,13},{6,14},{7,15},{8,0},{9,1},... | collective-permute-start | bytes 1867784 | tf_op jit(solution)/shard_map/ppermute | solution.py:54
  82.9 0.3 pad_maximum_fusion.refs_8_
  83.2 0.1 collective-permute-start.17
  83.3 10.9 %collective-permute-done.9.refs_10_ = bf16[304,1024]{1,0:T(8,128)(2,1)S(1)} collective-permute-done((bf16[304,1024]{1,0:T(8,128)(2,1)S(1)}, bf16[304,1024]{1,0:T(8,128)(2,1)S(1)}, u32[]{:S(2)}, u32[]{:S(2)}) %collective-permute-start.9) | collective-permute-done | bytes 622624 | tf_op jit(solution)/shard_map/ppermute | solution.py:54
  94.3 1.2 collective-permute-done.13.refs_20_
  95.5 0.5 collective-permute-start.18
  96.0 2.5 %collective-permute-done.4.refs_7_ = bf16[608,1408]{1,0:T(8,128)(2,1)} collective-permute-done((bf16[608,1408]{1,0:T(8,128)(2,1)S(1)}, bf16[608,1408]{1,0:T(8,128)(2,1)}, u32[]{:S(2)}, u32[]{:S(2)}) %collective-permute-start.4) | collective-permute-done | bytes 1712160 | tf_op jit(solution)/shard_map/ppermute | solution.py:72
  98.5 0.6 collective-permute-start.14
  99.1 0.7 copy-done.5
  99.8 0.8 copy-done.7
  100.6 0.5 collective-permute-start.16
  101.1 0.6 copy.26
  101.8 0.7 broadcast_in_dim_tile.3.refs_3_
  102.5 0.7 stack.52.refs_0_
  103.2 2.3 collective-permute-done.14.refs_12_
  105.4 2.4 %collective-permute-done.16.refs_14_ = bf16[608,1408]{1,0:T(8,128)(2,1)} collective-permute-done((bf16[608,1408]{1,0:T(8,128)(2,1)}, bf16[608,1408]{1,0:T(8,128)(2,1)}, u32[]{:S(2)}, u32[]{:S(2)}) %collective-permute-start.16) | collective-permute-done | bytes 1712160 | tf_op jit(solution)/shard_map/ppermute | solution.py:58
  107.9 26.8 %first_layer.3 = (bf16[256,2432]{1,0:T(8,128)(2,1)}, bf16[256,2432]{1,0:T(8,128)(2,1)}) custom-call(s32[10]{0:T(128)} %stack.52.refs_0_, bf16[2,256,2432]{2,1,0:T(8,128)(2,1)} %refs_1_.3, f32[2,3,2432]{2,1,0:T(4,128)} %bitcast.33, f32[1,1280]{1,0:T(1,128)} %broadcast_in_dim_tile.3.refs_3_, bf16[608,1408]{1,0:T(8,128)(2,1)} %copy-done.3, ...), custom_call_target="tpu_custom_call" | custom-call | tf_op jit(solution)/shard_map/first_layer/pallas_call | solution.py:359
  134.7 4.1 %collective-permute-start.21 = (bf16[256,2432]{1,0:T(8,128)(2,1)}, bf16[256,2432]{1,0:T(8,128)(2,1)S(1)}, u32[]{:S(2)}, u32[]{:S(2)}) collective-permute-start(bf16[256,2432]{1,0:T(8,128)(2,1)} %get-tuple-element.35), channel_id=1, source_target_pairs={{0,64},{1,65},{2,66},{3,67},{4,68},{5,69},{6,70},{7,71},{8,72},{9,... | collective-permute-start | bytes 3735560 | tf_op jit(solution)/shard_map/ppermute | solution.py:437
  138.8 26.6 %first_layer.2 = (bf16[256,2432]{1,0:T(8,128)(2,1)}, bf16[256,2432]{1,0:T(8,128)(2,1)}) custom-call(s32[10]{0:T(128)} %stack.52.refs_0_, bf16[2,256,2432]{2,1,0:T(8,128)(2,1)} %refs_1_.3, f32[2,3,2432]{2,1,0:T(4,128)} %bitcast.34, f32[1,1280]{1,0:T(1,128)} %broadcast_in_dim_tile.3.refs_3_, bf16[608,1408]{1,0:T(8,128)(2,1)} %copy-done.3, ...), custom_call_target="tpu_custom_call" | custom-call | tf_op jit(solution)/shard_map/first_layer/pallas_call | solution.py:359
  165.4 1.4 collective-permute-start.20
  166.8 1.1 copy.18.refs_23_
  167.9 1.0 copy-done.12
  169.0 29.5 %last_layer.2 = (bf16[128,64]{1,0:T(8,128)(2,1)}, bf16[2,256,2432]{2,1,0:T(8,128)(2,1)}, f32[128,64]{1,0:T(8,128)}) custom-call(s32[10]{0:T(128)} %stack.52.refs_0_, bf16[256,2432]{1,0:T(8,128)(2,1)} %copy-done.12, f32[2,3,2432]{2,1,0:T(4,128)} %bitcast.35, f32[1,1280]{1,0:T(1,128)} %broadcast_in_dim_tile.3.refs_3_, bf16[608,1408]{1,0:T(8,128)(2,1)} %copy-done.3, ...), custom_call_target="tpu_custom_call" | custom-call | tf_op jit(solution)/shard_map/last_layer/pallas_call | solution.py:359
  198.5 1.3 collective-permute-start.22
  199.8 0.1 copy.19
  199.9 1.1 copy-done.11
  201.0 29.3 %last_layer.3 = (bf16[128,64]{1,0:T(8,128)(2,1)}, bf16[2,256,2432]{2,1,0:T(8,128)(2,1)}, f32[128,64]{1,0:T(8,128)}) custom-call(s32[10]{0:T(128)} %stack.52.refs_0_, bf16[256,2432]{1,0:T(8,128)(2,1)} %copy-done.11, f32[2,3,2432]{2,1,0:T(4,128)} %bitcast.36, f32[1,1280]{1,0:T(1,128)} %broadcast_in_dim_tile.3.refs_3_, ...), custom_call_target="tpu_custom_call", output_to_operand_aliasing={{1}: (25, {})} | custom-call | tf_op jit(solution)/shard_map/last_layer/pallas_call | solution.py:359
  230.2 1.3 collective-permute-start.23
  231.6 4.7 %collective-permute-done.23 = bf16[128,64]{1,0:T(8,128)(2,1)S(1)} collective-permute-done((bf16[128,64]{1,0:T(8,128)(2,1)}, bf16[128,64]{1,0:T(8,128)(2,1)S(1)}, u32[]{:S(2)}, u32[]{:S(2)}) %collective-permute-start.23) | collective-permute-done | bytes 16416 | tf_op jit(solution)/shard_map/ppermute | solution.py:441
  236.3 0.1 multiply_subtract_fusion
  236.4 0.7 copy.21
  237.1 0.7 copy.22
  (52 shorter events, 0.2 us)
Async XLA Ops:
  0.6 6.4 %copy-start.8 = (bf16[1,152,3648]{2,1,0:T(8,128)(2,1)S(1)}, bf16[1,152,3648]{2,1,0:T(8,128)(2,1)}, u32[]{:S(2)}) copy-start(bf16[1,152,3648]{2,1,0:T(8,128)(2,1)} %param.16) | copy-start | bytes 3326980
  0.6 6.4 %copy-start.9 = (bf16[1,1216,152]{1,2,0:T(8,128)(2,1)S(1)}, bf16[1,1216,152]{1,2,0:T(8,128)(2,1)}, u32[]{:S(2)}) copy-start(bf16[1,1216,152]{1,2,0:T(8,128)(2,1)} %param.17) | copy-start | bytes 1108996
  3.6 3.4 %collective-permute-start = (bf16[152,2432]{1,0:T(8,128)(2,1)S(1)}, bf16[152,2432]{1,0:T(8,128)(2,1)S(1)}, u32[]{:S(2)}, u32[]{:S(2)}) collective-permute-start(bf16[152,2432]{1,0:T(8,128)(2,1)S(1)} %broadcast_select_fusion.4), channel_id=1, source_target_pairs={{0,1},{1,0},{2,3},{3,2},{4,5},{5,4},{6,7},{7,6},{8,9},{9,8},{10,11... | collective-permute-start | bytes 2217992 | tf_op jit(solution)/shard_map/ppermute | solution.py:58
  3.7 58.0 %collective-permute-start.11 = (bf16[2,256,2432]{2,1,0:T(8,128)(2,1)}, bf16[2,256,2432]{2,1,0:T(8,128)(2,1)S(1)}, u32[]{:S(2)}, u32[]{:S(2)}) collective-permute-start(bf16[2,256,2432]{2,1,0:T(8,128)(2,1)} %bitcast.39), channel_id=1, source_target_pairs={{0,16},{16,32},{32,48},{48,0},{1,17},{17,33},{33,49},{49,1},{2,18}... | collective-permute-start | bytes 7471112 | tf_op jit(solution)/shard_map/ppermute | solution.py:62
  5.5 56.3 %collective-permute-start.12 = (bf16[2,256,2432]{2,1,0:T(8,128)(2,1)}, bf16[2,256,2432]{2,1,0:T(8,128)(2,1)S(1)}, u32[]{:S(2)}, u32[]{:S(2)}) collective-permute-start(bf16[2,256,2432]{2,1,0:T(8,128)(2,1)} %bitcast.40), channel_id=1, source_target_pairs={{0,48},{16,0},{32,16},{48,32},{1,49},{17,1},{33,17},{49,33},{2,50}... | collective-permute-start | bytes 7471112 | tf_op jit(solution)/shard_map/ppermute | solution.py:62
  7.8 7.5 %copy-start.10 = (bf16[1,2,154,2432]{3,1,2,0:T(2,128)(2,1)S(1)}, bf16[1,2,154,2432]{3,1,2,0:T(2,128)(2,1)}, u32[]{:S(2)}) copy-start(bf16[1,2,154,2432]{3,1,2,0:T(2,128)(2,1)} %param.12) | copy-start | bytes 4494340
  7.9 17.2 %collective-permute-start.5 = (bf16[304,1024]{1,0:T(8,128)(2,1)S(1)}, bf16[304,1024]{1,0:T(8,128)(2,1)S(1)}, u32[]{:S(2)}, u32[]{:S(2)}) collective-permute-start(bf16[304,1024]{1,0:T(8,128)(2,1)S(1)} %pad_maximum_fusion.4), channel_id=1, source_target_pairs={{0,2},{1,3},{2,4},{3,5},{4,6},{5,7},{6,0},{7,1},{8,10},{9,11},{10,... | collective-permute-start | bytes 1867784 | tf_op jit(solution)/shard_map/ppermute | solution.py:50
  9.6 15.6 %collective-permute-start.6 = (bf16[304,1024]{1,0:T(8,128)(2,1)S(1)}, bf16[304,1024]{1,0:T(8,128)(2,1)S(1)}, u32[]{:S(2)}, u32[]{:S(2)}) collective-permute-start(bf16[304,1024]{1,0:T(8,128)(2,1)S(1)} %pad_maximum_fusion.4), channel_id=1, source_target_pairs={{0,6},{1,7},{2,0},{3,1},{4,2},{5,3},{6,4},{7,5},{8,14},{9,15},{10,... | collective-permute-start | bytes 1867784 | tf_op jit(solution)/shard_map/ppermute | solution.py:50
  11.3 22.6 %collective-permute-start.1 = (bf16[304,1408]{1,0:T(8,128)(2,1)S(1)}, bf16[304,1408]{1,0:T(8,128)(2,1)S(1)}, u32[]{:S(2)}, u32[]{:S(2)}) collective-permute-start(bf16[304,1408]{1,0:T(8,128)(2,1)S(1)} %fusion), channel_id=1, source_target_pairs={{0,8},{1,9},{2,10},{3,11},{4,12},{5,13},{6,14},{7,15},{8,0},{9,1},... | collective-permute-start | bytes 2568200 | tf_op jit(solution)/shard_map/ppermute | solution.py:54
  25.2 12.3 %collective-permute-start.7 = (bf16[304,1024]{1,0:T(8,128)(2,1)S(1)}, bf16[304,1024]{1,0:T(8,128)(2,1)S(1)}, u32[]{:S(2)}, u32[]{:S(2)}) collective-permute-start(bf16[304,1024]{1,0:T(8,128)(2,1)S(1)} %broadcast_select_fusion.6), channel_id=1, source_target_pairs={{0,2},{1,7},{2,4},{3,1},{4,6},{5,3},{6,0},{7,5},{8,10},{9,15},{10,... | collective-permute-start | bytes 1867784 | tf_op jit(solution)/shard_map/ppermute | solution.py:72
  34.0 41.5 %copy-start.3 = (bf16[608,1408]{1,0:T(8,128)(2,1)}, bf16[608,1408]{1,0:T(8,128)(2,1)S(1)}, u32[]{:S(2)}) copy-start(bf16[608,1408]{1,0:T(8,128)(2,1)S(1)} %pad_maximum_fusion.2.refs_4_) | copy-start | bytes 5136388
  34.0 39.5 %collective-permute-start.2 = (bf16[608,1408]{1,0:T(8,128)(2,1)S(1)}, bf16[608,1408]{1,0:T(8,128)(2,1)}, u32[]{:S(2)}, u32[]{:S(2)}) collective-permute-start(bf16[608,1408]{1,0:T(8,128)(2,1)S(1)} %pad_maximum_fusion.2.refs_4_), channel_id=1, source_target_pairs={{0,2},{1,3},{2,4},{3,5},{4,6},{5,7},{6,0},{7,1},{8,10},{9,11},{10,... | collective-permute-start | bytes 5136392 | tf_op jit(solution)/shard_map/ppermute | solution.py:50
  34.4 39.1 %collective-permute-start.3 = (bf16[608,1408]{1,0:T(8,128)(2,1)S(1)}, bf16[608,1408]{1,0:T(8,128)(2,1)}, u32[]{:S(2)}, u32[]{:S(2)}) collective-permute-start(bf16[608,1408]{1,0:T(8,128)(2,1)S(1)} %pad_maximum_fusion.2.refs_4_), channel_id=1, source_target_pairs={{0,6},{1,7},{2,0},{3,1},{4,2},{5,3},{6,4},{7,5},{8,14},{9,15},{10,... | collective-permute-start | bytes 5136392 | tf_op jit(solution)/shard_map/ppermute | solution.py:50
  37.5 42.5 %collective-permute-start.8 = (bf16[912,1024]{1,0:T(8,128)(2,1)S(1)}, bf16[912,1024]{1,0:T(8,128)(2,1)}, u32[]{:S(2)}, u32[]{:S(2)}) collective-permute-start(bf16[912,1024]{1,0:T(8,128)(2,1)S(1)} %pad_maximum_fusion.1), channel_id=1, source_target_pairs={{0,8},{1,9},{2,10},{3,11},{4,12},{5,13},{6,14},{7,15},{8,0},{9,1},... | collective-permute-start | bytes 5603336 | tf_op jit(solution)/shard_map/ppermute | solution.py:54
  61.8 1.5 copy-start.1
  61.8 2.2 copy-start.2
  64.0 31.5 %collective-permute-start.13 = (bf16[2,256,2432]{2,1,0:T(8,128)(2,1)S(1)}, bf16[2,256,2432]{2,1,0:T(8,128)(2,1)S(1)}, u32[]{:S(2)}, u32[]{:S(2)}) collective-permute-start(bf16[2,256,2432]{2,1,0:T(8,128)(2,1)S(1)} %broadcast_select_fusion), channel_id=1, source_target_pairs={{0,16},{1,49},{2,18},{3,51},{4,20},{5,53},{6,22},{7,55},{8,24},{9,... | collective-permute-start | bytes 7471112 | tf_op jit(solution)/shard_map/ppermute | solution.py:81
  75.2 26.0 %copy-start.16 = (f32[1,2,3,2432]{3,1,2,0:T(2,128)S(1)}, f32[1,2,3,2432]{3,1,2,0:T(2,128)}, u32[]{:S(2)}) copy-start(f32[1,2,3,2432]{3,1,2,0:T(2,128)} %param.14) | copy-start | bytes 175108
  75.2 26.6 %copy-start.17 = (f32[1,64]{1,0:T(1,128)S(1)}, f32[1,64]{1,0:T(1,128)}, u32[]{:S(2)}) copy-start(f32[1,64]{1,0:T(1,128)} %param.15) | copy-start | bytes 772
  75.2 23.3 %collective-permute-start.4 = (bf16[608,1408]{1,0:T(8,128)(2,1)S(1)}, bf16[608,1408]{1,0:T(8,128)(2,1)}, u32[]{:S(2)}, u32[]{:S(2)}) collective-permute-start(bf16[608,1408]{1,0:T(8,128)(2,1)S(1)} %broadcast_select_fusion.1), channel_id=1, source_target_pairs={{0,2},{1,7},{2,4},{3,1},{4,6},{5,3},{6,0},{7,5},{8,10},{9,15},{10,... | collective-permute-start | bytes 5136392 | tf_op jit(solution)/shard_map/ppermute | solution.py:72
  75.5 23.0 %collective-permute-start.10 = (bf16[608,1408]{1,0:T(8,128)(2,1)S(1)}, bf16[608,1408]{1,0:T(8,128)(2,1)S(1)}, u32[]{:S(2)}, u32[]{:S(2)}) collective-permute-start(bf16[608,1408]{1,0:T(8,128)(2,1)S(1)} %pad_maximum_fusion.2.refs_4_), channel_id=1, source_target_pairs={{0,1},{1,0},{2,3},{3,2},{4,5},{5,4},{6,7},{7,6},{8,9},{9,8},{10,11... | collective-permute-start | bytes 5136392 | tf_op jit(solution)/shard_map/ppermute | solution.py:58
  80.0 14.3 %collective-permute-start.9 = (bf16[304,1024]{1,0:T(8,128)(2,1)S(1)}, bf16[304,1024]{1,0:T(8,128)(2,1)S(1)}, u32[]{:S(2)}, u32[]{:S(2)}) collective-permute-start(bf16[304,1024]{1,0:T(8,128)(2,1)S(1)} %collective-permute-done.7), channel_id=1, source_target_pairs={{0,8},{1,9},{2,10},{3,11},{4,12},{5,13},{6,14},{7,15},{8,0},{9,1},... | collective-permute-start | bytes 1867784 | tf_op jit(solution)/shard_map/ppermute | solution.py:54
  83.2 24.7 %copy-start = (bf16[1216,1024]{1,0:T(8,128)(2,1)}, bf16[1216,1024]{1,0:T(8,128)(2,1)S(1)}, u32[]{:S(2)}) copy-start(bf16[1216,1024]{1,0:T(8,128)(2,1)S(1)} %pad_maximum_fusion.refs_8_) | copy-start | bytes 7471108
  83.2 19.9 %collective-permute-start.17 = (bf16[1216,1024]{1,0:T(8,128)(2,1)S(1)}, bf16[1216,1024]{1,0:T(8,128)(2,1)}, u32[]{:S(2)}, u32[]{:S(2)}) collective-permute-start(bf16[1216,1024]{1,0:T(8,128)(2,1)S(1)} %pad_maximum_fusion.refs_8_), channel_id=1, source_target_pairs={{0,1},{1,0},{2,3},{3,2},{4,5},{5,4},{6,7},{7,6},{8,9},{9,8},{10,11... | collective-permute-start | bytes 7471112 | tf_op jit(solution)/shard_map/ppermute | solution.py:58
  94.3 13.6 %copy-start.6 = (bf16[304,1024]{1,0:T(8,128)(2,1)}, bf16[304,1024]{1,0:T(8,128)(2,1)S(1)}, u32[]{:S(2)}) copy-start(bf16[304,1024]{1,0:T(8,128)(2,1)S(1)} %collective-permute-done.9.refs_10_) | copy-start | bytes 1867780
  95.5 3.0 %copy-start.4 = (bf16[2,256,2432]{2,1,0:T(8,128)(2,1)}, bf16[2,256,2432]{2,1,0:T(8,128)(2,1)S(1)}, u32[]{:S(2)}) copy-start(bf16[2,256,2432]{2,1,0:T(8,128)(2,1)S(1)} %collective-permute-done.13.refs_20_) | copy-start | bytes 7471108
  95.5 4.3 %collective-permute-start.19 = (bf16[304,1024]{1,0:T(8,128)(2,1)S(1)}, bf16[304,1024]{1,0:T(8,128)(2,1)S(1)}, u32[]{:S(2)}, u32[]{:S(2)}) collective-permute-start(bf16[304,1024]{1,0:T(8,128)(2,1)S(1)} %collective-permute-done.9.refs_10_), channel_id=1, source_target_pairs={{0,1},{1,0},{2,3},{3,2},{4,5},{5,4},{6,7},{7,6},{8,9},{9,8},{10,11... | collective-permute-start | bytes 1867784 | tf_op jit(solution)/shard_map/ppermute | solution.py:58
  95.5 12.4 %collective-permute-start.18 = (bf16[912,1024]{1,0:T(8,128)(2,1)}, bf16[912,1024]{1,0:T(8,128)(2,1)}, u32[]{:S(2)}, u32[]{:S(2)}) collective-permute-start(bf16[912,1024]{1,0:T(8,128)(2,1)} %collective-permute-done.8.refs_9_), channel_id=1, source_target_pairs={{0,1},{1,0},{2,3},{3,2},{4,5},{5,4},{6,7},{7,6},{8,9},{9,8},{10,11... | collective-permute-start | bytes 5603336 | tf_op jit(solution)/shard_map/ppermute | solution.py:58
  98.5 4.7 %collective-permute-start.15 = (bf16[608,1408]{1,0:T(8,128)(2,1)}, bf16[608,1408]{1,0:T(8,128)(2,1)}, u32[]{:S(2)}, u32[]{:S(2)}) collective-permute-start(bf16[608,1408]{1,0:T(8,128)(2,1)} %collective-permute-done.3.refs_6_), channel_id=1, source_target_pairs={{0,1},{1,0},{2,3},{3,2},{4,5},{5,4},{6,7},{7,6},{8,9},{9,8},{10,11... | collective-permute-start | bytes 5136392 | tf_op jit(solution)/shard_map/ppermute | solution.py:58
  98.5 1.3 copy-start.5
  98.5 6.9 %collective-permute-start.14 = (bf16[608,1408]{1,0:T(8,128)(2,1)}, bf16[608,1408]{1,0:T(8,128)(2,1)}, u32[]{:S(2)}, u32[]{:S(2)}) collective-permute-start(bf16[608,1408]{1,0:T(8,128)(2,1)} %collective-permute-done.2.refs_5_), channel_id=1, source_target_pairs={{0,1},{1,0},{2,3},{3,2},{4,5},{5,4},{6,7},{7,6},{8,9},{9,8},{10,11... | collective-permute-start | bytes 5136392 | tf_op jit(solution)/shard_map/ppermute | solution.py:58
  99.8 0.8 copy-start.7
  100.6 7.3 %collective-permute-start.16 = (bf16[608,1408]{1,0:T(8,128)(2,1)}, bf16[608,1408]{1,0:T(8,128)(2,1)}, u32[]{:S(2)}, u32[]{:S(2)}) collective-permute-start(bf16[608,1408]{1,0:T(8,128)(2,1)} %collective-permute-done.4.refs_7_), channel_id=1, source_target_pairs={{0,1},{1,0},{2,3},{3,2},{4,5},{5,4},{6,7},{7,6},{8,9},{9,8},{10,11... | collective-permute-start | bytes 5136392 | tf_op jit(solution)/shard_map/ppermute | solution.py:58
  134.7 32.1 %copy-start.13 = (bf16[2432,64]{0,1:T(8,128)(2,1)S(1)}, bf16[2432,64]{0,1:T(8,128)(2,1)}, u32[]{:S(2)}) copy-start(bf16[2432,64]{0,1:T(8,128)(2,1)} %param.19) | copy-start | bytes 933892
  134.7 33.2 %collective-permute-start.21 = (bf16[256,2432]{1,0:T(8,128)(2,1)}, bf16[256,2432]{1,0:T(8,128)(2,1)S(1)}, u32[]{:S(2)}, u32[]{:S(2)}) collective-permute-start(bf16[256,2432]{1,0:T(8,128)(2,1)} %get-tuple-element.35), channel_id=1, source_target_pairs={{0,64},{1,65},{2,66},{3,67},{4,68},{5,69},{6,70},{7,71},{8,72},{9,... | collective-permute-start | bytes 3735560 | tf_op jit(solution)/shard_map/ppermute | solution.py:437
  165.4 34.5 %collective-permute-start.20 = (bf16[256,2432]{1,0:T(8,128)(2,1)}, bf16[256,2432]{1,0:T(8,128)(2,1)S(1)}, u32[]{:S(2)}, u32[]{:S(2)}) collective-permute-start(bf16[256,2432]{1,0:T(8,128)(2,1)} %get-tuple-element.33), channel_id=1, source_target_pairs={{0,64},{1,65},{2,66},{3,67},{4,68},{5,69},{6,70},{7,71},{8,72},{9,... | collective-permute-start | bytes 3735560 | tf_op jit(solution)/shard_map/ppermute | solution.py:437
  167.9 1.0 copy-start.12
  169.0 30.8 %copy-start.18 = (s32[2]{0:T(128)S(1)}, s32[2]{0:T(128)}, u32[]{:S(2)}) copy-start(s32[2]{0:T(128)} %param.21) | copy-start | bytes 28
  169.0 30.8 %copy-start.14 = (f32[2,128,64]{1,2,0:T(8,128)S(1)}, f32[2,128,64]{1,2,0:T(8,128)}, u32[]{:S(2)}) copy-start(f32[2,128,64]{1,2,0:T(8,128)} %param.20) | copy-start | bytes 196612
  198.5 33.1 %collective-permute-start.22 = (bf16[128,64]{1,0:T(8,128)(2,1)}, bf16[128,64]{1,0:T(8,128)(2,1)S(1)}, u32[]{:S(2)}, u32[]{:S(2)}) collective-permute-start(bf16[128,64]{1,0:T(8,128)(2,1)} %get-tuple-element.39), channel_id=1, source_target_pairs={{64,0},{65,1},{66,2},{67,3},{68,4},{69,5},{70,6},{71,7},{72,8},{73... | collective-permute-start | bytes 49160 | tf_op jit(solution)/shard_map/ppermute | solution.py:441
  199.9 1.1 copy-start.11
  201.0 30.6 %copy-start.15 = (f32[128,64]{1,0:T(8,128)S(1)}, f32[128,64]{1,0:T(8,128)}, u32[]{:S(2)}) copy-start(f32[128,64]{1,0:T(8,128)} %get-tuple-element.40) | copy-start | bytes 98308
  230.2 6.0 %collective-permute-start.23 = (bf16[128,64]{1,0:T(8,128)(2,1)}, bf16[128,64]{1,0:T(8,128)(2,1)S(1)}, u32[]{:S(2)}, u32[]{:S(2)}) collective-permute-start(bf16[128,64]{1,0:T(8,128)(2,1)} %get-tuple-element.41), channel_id=1, source_target_pairs={{64,0},{65,1},{66,2},{67,3},{68,4},{69,5},{70,6},{71,7},{72,8},{73... | collective-permute-start | bytes 49160 | tf_op jit(solution)/shard_map/ppermute | solution.py:441
